TPU v7x, 1024 devices: a whole 8x8x8 slice. The times are simulated.
1024 devices in a mesh: dp: 64 (over z_hi, x, core), seq: 16 (over z_lo, y).
Axes of the slice: x: 8, y: 8, z: 8 (z_hi: 4, z_lo: 2; z = z_hi * 2 + z_lo), core: 2. Of those that a mesh axis runs over, the one named last changes fastest.
Arguments:
- qkv: bfloat16 [131072, 3, 1152], P(('dp', 'seq')), may hold values from -6 to 6
- attn_out: bfloat16 [131072, 1152], P(('dp', 'seq')), may hold values from -24 to 24
- dout: bfloat16 [131072, 1152], P(('dp', 'seq')), may hold values from -16 to 16
- w_master: float32 [1152, 1152], P('dp', 'seq'), may hold values from -0.1875 to 0.1875
- mom1: float32 [1152, 1152], P('dp', 'seq'), may hold values from -6 to 6
- mom2: float32 [1152, 1152], P('dp', 'seq'), may hold values from 0.5 to 50
- grad_prev: float32 [1152, 1152], P('dp', 'seq'), may hold values from -16 to 16
Outputs:
- dqkv: bfloat16 [131072, 3, 1152], P(('dp', 'seq'))
- grad_new: float32 [1152, 1152], P('dp', 'seq')
- weight_new: float32 [1152, 1152], P('dp', 'seq')
- moment_one: float32 [1152, 1152], P('dp', 'seq')
- moment_two: float32 [1152, 1152], P('dp', 'seq')
All inputs are finite; a program needn't handle non-finite values.
Results may differ from a plain program's by a relative error of at most 0.02.
Values may be sent and summed in bfloat16 or wider, within the bound.
No kernel may reach another device: no remote copies, remote signals or barrier semaphores. Data moves between devices by JAX's collectives and lax.ppermute only.
A program may use at most 64 MiB of HBM per device.

v0:
```python
import jax
import jax.numpy as jnp
from jax import lax
from jax.sharding import PartitionSpec as P

HD = 72


BETA_ONE = 0.9
BETA_TWO = 0.999
LEARN_RATE = 0.001
ADAM_EPS = 1e-08
CORRECT_ONE = 0.999973438601112
CORRECT_TWO = 0.0952078528862904


def attend_backward(heads_qkv, heads_grad):
    seq_len = heads_qkv.shape[0]
    local_width = heads_qkv.shape[2]
    local_heads = local_width // HD
    factor = HD ** (-0.5)
    queries = heads_qkv[:, 0].reshape(seq_len, local_heads, HD)
    key_rows = heads_qkv[:, 1].reshape(seq_len, local_heads, HD)
    value_rows = heads_qkv[:, 2].reshape(seq_len, local_heads, HD)
    grad_rows = heads_grad[:, 0].reshape(seq_len, local_heads, HD)
    block_rows = min(512, seq_len)
    block_count = seq_len // block_rows

    def block_step(carry, number):
        keys_acc, values_acc = carry
        offset = number * block_rows
        query_block = lax.dynamic_slice_in_dim(queries, offset, block_rows, 0)
        grad_block = lax.dynamic_slice_in_dim(grad_rows, offset, block_rows, 0)
        scores = (
            jnp.einsum("qhd,khd->hqk", query_block, key_rows, preferred_element_type=jnp.float32)
            * factor
        )
        row_max = jnp.max(scores, axis=-1, keepdims=True)
        exponent = jnp.exp(scores - row_max)
        attention = exponent / jnp.sum(exponent, axis=-1, keepdims=True)
        attn_half = attention.astype(jnp.bfloat16)
        grad_probs = jnp.einsum(
            "qhd,khd->hqk", grad_block, value_rows, preferred_element_type=jnp.float32
        )
        row_dot = jnp.sum(attention * grad_probs, axis=-1, keepdims=True)
        grad_logits = (attention * (grad_probs - row_dot) * factor).astype(jnp.bfloat16)
        grad_query = jnp.einsum(
            "hqk,khd->qhd", grad_logits, key_rows, preferred_element_type=jnp.float32
        )
        keys_acc = keys_acc + jnp.einsum(
            "hqk,qhd->khd", grad_logits, query_block, preferred_element_type=jnp.float32
        )
        values_acc = values_acc + jnp.einsum(
            "hqk,qhd->khd", attn_half, grad_block, preferred_element_type=jnp.float32
        )
        return ((keys_acc, values_acc), grad_query.astype(jnp.bfloat16))

    zeros_acc = jnp.zeros((seq_len, local_heads, HD), jnp.float32)
    (keys_acc, values_acc), query_blocks = lax.scan(
        block_step, (zeros_acc, zeros_acc), jnp.arange(block_count)
    )
    grad_query = query_blocks.reshape(seq_len, local_heads, HD)
    stacked = jnp.stack(
        [grad_query, keys_acc.astype(jnp.bfloat16), values_acc.astype(jnp.bfloat16)], axis=1
    )
    return stacked.reshape(seq_len, 3, local_width)


def per_device(qkv, attn_out, dout, w_master, mom1, mom2, grad_prev):
    moment_one = BETA_ONE * mom1 + (1.0 - BETA_ONE) * grad_prev
    moment_two = BETA_TWO * mom2 + (1.0 - BETA_TWO) * grad_prev * grad_prev
    weight_new = w_master - LEARN_RATE * (moment_one / CORRECT_ONE) / (
        jnp.sqrt(moment_two / CORRECT_TWO) + ADAM_EPS
    )
    weight_half = weight_new.astype(jnp.bfloat16)
    dp_count = lax.axis_size("dp")
    seq_count = lax.axis_size("seq")
    heads_qkv = lax.all_to_all(qkv, "seq", split_axis=2, concat_axis=0, tiled=True)
    row_block = lax.all_gather(weight_half, "seq", axis=1, tiled=True)
    full_weight = lax.all_gather(row_block, "dp", axis=0, tiled=True)
    attn_grad = lax.dot_general(
        dout, full_weight, (((1,), (1,)), ((), ())), preferred_element_type=jnp.float32
    ).astype(jnp.bfloat16)
    grad_three = attn_grad[:, None, :]
    heads_grad = lax.all_to_all(grad_three, "seq", split_axis=2, concat_axis=0, tiled=True)
    local_grads = attend_backward(heads_qkv, heads_grad)
    dqkv = lax.all_to_all(local_grads, "seq", split_axis=0, concat_axis=2, tiled=True)
    total_tokens = dout.shape[0] * seq_count * dp_count
    factor = float(total_tokens) ** (-0.5)
    column_sums = lax.psum_scatter(
        (
            lax.dot_general(
                dout, attn_out, (((0,), (0,)), ((), ())), preferred_element_type=jnp.float32
            )
            * factor
        ).astype(jnp.bfloat16),
        "seq",
        scatter_dimension=0,
        tiled=True,
    ).astype(jnp.float32)
    block_sums = lax.psum_scatter(column_sums, "dp", scatter_dimension=1, tiled=True)
    grad_new = block_sums.T
    return (dqkv, grad_new, weight_new, moment_one, moment_two)


def solution(mesh):
    return jax.shard_map(
        per_device,
        mesh=mesh,
        in_specs=(
            P(("dp", "seq"), None, None),
            P(("dp", "seq"), None),
            P(("dp", "seq"), None),
            P("dp", "seq"),
            P("dp", "seq"),
            P("dp", "seq"),
            P("dp", "seq"),
        ),
        out_specs=(
            P(("dp", "seq"), None, None),
            P("dp", "seq"),
            P("dp", "seq"),
            P("dp", "seq"),
            P("dp", "seq"),
        ),
        check_vma=False,
    )
```

profile of v0, /device:TPU:1, one launch (start us, length us, event | category | flops | bytes accessed | tf_op | source)
XLA Modules:
  0.0 555.6 jit_solution(18004076288387959446)
XLA Ops:
  8.1 1.4 convert_bitcast_fusion.2
  9.5 30.6 %all-gather = bf16[16,72,18]{1,2,0:T(8,128)(2,1)S(1)} all-gather(bf16[1,72,18]{1,2,0:T(8,128)(2,1)S(1)} %get-tuple-element.130), channel_id=1, replica_groups=mesh['dp'=64,'seq'=16] {'seq'}, dimensions={0}, use_global_device_ids=true | all-gather | bytes 44064 | tf_op jit(solution)/shard_map/all_gather | solution.py:79
  40.1 0.8 reshape.69
  40.9 3.2 copy.41
  44.1 3.7 all-to-all-start
  47.8 99.4 %all-gather.4.cloned.1.call-done = bf16[64,18,1152]{2,1,0:T(8,128)(2,1)} async-done(((bf16[1,18,1152]{2,1,0:T(8,128)(2,1)}), bf16[64,18,1152]{2,1,0:T(8,128)(2,1)}) %all-gather.4.cloned.1.call-update) | async-done | bytes 2654224 | tf_op jit(solution)/shard_map/all_gather | solution.py:80
  147.2 5.4 reshape.71
  152.6 2.6 fusion.26
  155.2 4.6 copy.65
  160.4 6.8 %reduce.6 = bf16[1152,128]{1,0:T(8,128)(2,1)S(1)} reduce(bf16[1152,1,128]{2,1,0:T(2,128)(2,1)S(1)} %bitcast.135, bf16[]{:T(256)} %broadcast.47), dimensions={1}, to_apply=%bitcast.104.reduce_sub_computation | reduce | bytes 589826
  167.1 0.8 reshape.80
  167.9 6.8 %all-to-all-start.1 = ((bf16[16,2,4608]{2,1,0:T(2,128)(2,1)}), bf16[16,2,4608]{2,1,0:T(2,128)(2,1)S(1)}, u32[]{:S(2)}, u32[]{:S(2)}) async-start(bf16[16,2,4608]{2,1,0:T(2,128)(2,1)} %reshape.80), calls=%async_computation.1 | async-start | bytes 589824 | tf_op jit(solution)/shard_map/all_to_all | solution.py:85
  174.9 2.4 fusion.25
  177.9 6.5 %all-to-all-done.1 = bf16[16,2,4608]{2,1,0:T(2,128)(2,1)S(1)} async-done(((bf16[16,2,4608]{2,1,0:T(2,128)(2,1)}), bf16[16,2,4608]{2,1,0:T(2,128)(2,1)S(1)}, u32[]{:S(2)}, u32[]{:S(2)}) %all-to-all-start.1) | async-done | bytes 294944 | tf_op jit(solution)/shard_map/all_to_all | solution.py:85
  184.7 50.5 %while.15 = (s32[]{:T(128)}, f32[2048,1,72]{0,2,1:T(8,128)S(1)}, f32[2048,1,72]{0,2,1:T(8,128)S(1)}, bf16[4,512,1,72]{1,3,2,0:T(8,128)(2,1)S(1)}, s32[4]{0:T(128...) while((s32[]{:T(128)}, f32[2048,1,72]{0,2,1:T(8,128)S(1)}, ...), condition=%wide.region_4.5_spmd.clone, body=%wide.region_0.4_spmd.clone.sunk | while | flops 777619968 | bytes 72841488 | solution.py:59
  186.0 0.8 multiply_reduce_fusion.4
  186.8 1.9 copy-done.1
  188.7 0.8 fusion.52
  189.6 3.6 fusion.54
  193.2 1.4 multiply_reduce_fusion.5
  194.5 1.5 multiply_convert_fusion.2
  198.6 0.8 multiply_reduce_fusion.4
  199.5 1.9 copy-done.1
  201.4 0.8 fusion.52
  202.3 3.5 fusion.54
  205.8 1.4 multiply_reduce_fusion.5
  207.1 1.5 multiply_convert_fusion.2
  209.2 0.8 fusion.55
  211.2 0.8 multiply_reduce_fusion.4
  212.1 1.9 copy-done.1
  214.0 0.8 fusion.52
  214.8 3.5 fusion.54
  218.4 1.4 multiply_reduce_fusion.5
  219.7 1.5 multiply_convert_fusion.2
  223.8 0.8 multiply_reduce_fusion.4
  224.7 1.9 copy-done.1
  226.6 0.8 fusion.52
  227.4 3.5 fusion.54
  231.0 1.4 multiply_reduce_fusion.5
  232.3 1.5 multiply_convert_fusion.2
  235.7 1.4 copy.48
  237.1 3.7 reshape.82
  240.8 5.3 all-to-all-start.2
  246.1 1.3 dynamic-slice.2
  248.1 293.2 %all-reduce.3 = f32[72,1152]{1,0:T(8,128)S(1)} all-reduce(bf16[72,1152]{1,0:T(8,128)(2,1)} %reduce-scatter.6.cloned.1.call-done), channel_id=3, replica_groups=mesh['dp'=64,'seq'=16] {'dp'}, use_global_device_ids=true, to_apply=%region_6.7.clone | all-reduce | flops 82944 | bytes 497664
  542.1 3.3 reshape.83
  545.4 1.2 copy.54
  546.6 1.5 copy.51
  (52 shorter events, 9.9 us)
Async XLA Ops:
  8.0 144.6 %copy-start = (bf16[128,1152]{1,0:T(8,128)(2,1)S(1)}, bf16[128,1152]{1,0:T(8,128)(2,1)}, u32[]{:S(2)}) copy-start(bf16[128,1152]{1,0:T(8,128)(2,1)} %param.11) | copy-start | bytes 884740
  8.0 139.2 %all-gather.4.cloned.1.call-start = ((), (), s32[]{:S(2)}) async-start(), calls=%async_computation.4 | async-start | bytes 3594240 | tf_op jit(solution)/shard_map/all_gather | solution.py:80
  44.1 123.8 %all-to-all-start = ((bf16[128,3,1152]{0,1,2:T(4,128)(2,1)}), bf16[128,3,1152]{0,1,2:T(4,128)(2,1)S(1)}, u32[]{:S(2)}, u32[]{:S(2)}) async-start(bf16[128,3,1152]{0,1,2:T(4,128)(2,1)} %copy.41), calls=%async_computation | async-start | bytes 2359296 | tf_op jit(solution)/shard_map/all_to_all | solution.py:78
  152.6 22.3 %copy-start.3 = (bf16[128,1152]{1,0:T(8,128)(2,1)S(1)}, bf16[128,1152]{1,0:T(8,128)(2,1)}, u32[]{:S(2)}) copy-start(bf16[128,1152]{1,0:T(8,128)(2,1)} %param.10) | copy-start | bytes 884740
  167.9 16.4 %all-to-all-start.1 = ((bf16[16,2,4608]{2,1,0:T(2,128)(2,1)}), bf16[16,2,4608]{2,1,0:T(2,128)(2,1)S(1)}, u32[]{:S(2)}, u32[]{:S(2)}) async-start(bf16[16,2,4608]{2,1,0:T(2,128)(2,1)} %reshape.80), calls=%async_computation.1 | async-start | bytes 589824 | tf_op jit(solution)/shard_map/all_to_all | solution.py:85
  174.7 73.4 %reduce-scatter.6.cloned.1.call-start = ((), (), s32[]{:S(2)}) async-start(), calls=%async_computation.5 | async-start | bytes 2820096
  186.8 1.9 copy-start.1
  189.6 3.6 copy-start.2
  199.5 1.9 copy-start.1
  202.2 3.5 copy-start.2
  212.1 1.9 copy-start.1
  214.8 3.5 copy-start.2
  224.7 1.9 copy-start.1
  227.4 3.5 copy-start.2
  240.8 301.2 %all-to-all-start.2 = ((bf16[16,2,13824]{2,1,0:T(2,128)(2,1)}), bf16[16,2,13824]{2,1,0:T(2,128)(2,1)S(1)}, u32[]{:S(2)}, u32[]{:S(2)}) async-start(bf16[16,2,13824]{2,1,0:T(2,128)(2,1)} %reshape.82), calls=%async_computation.2 | async-start | bytes 1769472 | tf_op jit(solution)/shard_map/all_to_all | solution.py:87
Sparse Core Ops, SparseCore 0:
  41.0 106.1 all-gather.3
Sparse Core Ops, SparseCore 1:
  178.6 67.6 reduce-scatter.5
where the time goes:
time: 560 us; the launch traced here: 556 us
  blocking collectives  324 us (58%)
  waiting for transfers between devices  106 us (19%)
  local copies, waits for them, and re-layouts  39.8 us (7%)
  matrix products  33.2 us (6%)
  other arithmetic  17.7 us (3%)
  between operations  16.4 us (3%)
  starting transfers between devices  16 us (3%)
    unnamed x1, blocking collectives  293 us
    all_gather x1, waiting for transfers between devices, per_device(): full_weight = lax.all_gather(row_block, 'dp', axis=0, tiled=True)  99.4 us
    all_gather x1, blocking collectives, per_device(): row_block = lax.all_gather(weight_half, 'seq', axis=1, tiled=True)  30.6 us
    unnamed x16, local copies, waits for them, and re-layouts  21.5 us
    dot_general x4, matrix products, block_step(): jnp.einsum('hqk,qhd->khd', attn_half, grad_block, preferred_element_type=...  14.1 us
  transfers between devices with their start and end apart: 5, of which 2 were waited for; matrix products, arithmetic and copies ran while one was open for 13% of the time, Pallas kernels for 0%

commit v1 on v0

v1 whole, which is shorter than its diff:
```python
import jax
import jax.numpy as jnp
from jax import lax
from jax.experimental import pallas as pl
from jax.experimental.pallas import tpu as pltpu
from jax.sharding import Mesh, PartitionSpec as P

HD = 72
BLOCK = 256

BETA_ONE = 0.9
BETA_TWO = 0.999
LEARN_RATE = 0.001
ADAM_EPS = 1e-08
CORRECT_ONE = 0.999973438601112
CORRECT_TWO = 0.0952078528862904
LOG2_E = 1.4426950408889634


def probs_kernel(heads_ref, probs_ref, keys_ref):
    blocks = heads_ref.shape[0]
    width = heads_ref.shape[3]
    step = pl.program_id(0)

    @pl.when(step == 0)
    def _():
        for s in range(blocks):
            keys_ref[s * width : (s + 1) * width, :] = heads_ref[s, 1].T

    per = probs_ref.shape[1] // width
    queries = jnp.concatenate([heads_ref[step * per + j, 0] for j in range(per)], axis=1)
    scores = lax.dot_general(
        keys_ref[...], queries, (((1,), (0,)), ((), ())), preferred_element_type=jnp.float32
    )
    top = jnp.max(scores, axis=0, keepdims=True)
    weights = jnp.exp2((scores - top) * (HD ** (-0.5) * LOG2_E))
    total = jnp.sum(weights, axis=0, keepdims=True)
    probs_ref[...] = (weights * (1.0 / total)).astype(jnp.bfloat16)


def grads_kernel(
    heads_ref, grad_ref, probs_ref, out_ref, keys_ref, values_ref, grads_ref, dkeys_ref, dvalues_ref
):
    blocks = heads_ref.shape[0]
    width = heads_ref.shape[3]
    step = pl.program_id(0)
    per = probs_ref.shape[1] // width
    block = per * width
    factor = HD ** (-0.5)

    @pl.when(step == 0)
    def _():
        for s in range(blocks):
            keys_ref[:, s * width : (s + 1) * width] = heads_ref[s, 1]
            values_ref[s * width : (s + 1) * width, :] = heads_ref[s, 2].T
        dkeys_ref[...] = jnp.zeros_like(dkeys_ref)
        dvalues_ref[...] = jnp.zeros_like(dvalues_ref)
        count = HD // 2
        stride = grad_ref.shape[1] // 2
        dims = lax.broadcasted_iota(jnp.int32, (HD, stride), 0)
        order = lax.broadcasted_iota(jnp.int32, (HD, stride), 1)
        run = jnp.zeros_like(order)
        for k in range(1, count // SHARE):
            run += (order >= k * SHARE).astype(jnp.int32)
        side = blocks // 2
        parts = []
        for h in range(2):
            pieces = []
            for s in range(blocks):
                start = (h ^ (s // side)) * stride
                pieces.append(grad_ref[h * side + s % side, start : start + stride, :])
            choose = ((dims == order + SHARE * (run + h)) & (order < count)).astype(jnp.bfloat16)
            parts.append(
                lax.dot_general(
                    choose,
                    jnp.concatenate(pieces, axis=1),
                    (((1,), (0,)), ((), ())),
                    preferred_element_type=jnp.float32,
                )
            )
        placed = (parts[0] + parts[1]).astype(jnp.bfloat16)
        for b in range(pl.cdiv(blocks, per)):
            grads_ref[b] = placed[:, b * block : (b + 1) * block]

    grads_t = grads_ref[step]
    queries = jnp.concatenate([heads_ref[step * per + j, 0].T for j in range(per)], axis=0)
    half = probs_ref[...]
    grad_probs = lax.dot_general(
        values_ref[...], grads_t, (((1,), (0,)), ((), ())), preferred_element_type=jnp.float32
    )
    probs = half.astype(jnp.float32)
    row_dot = jnp.sum(probs * grad_probs, axis=0, keepdims=True)
    logits = (probs * (grad_probs - row_dot)).astype(jnp.bfloat16)
    dvalues_ref[...] += lax.dot_general(
        half, grads_t.T, (((1,), (0,)), ((), ())), preferred_element_type=jnp.float32
    )
    dkeys_ref[...] += lax.dot_general(
        logits, queries, (((1,), (0,)), ((), ())), preferred_element_type=jnp.float32
    )
    dqueries = factor * lax.dot_general(
        keys_ref[...], logits, (((1,), (0,)), ((), ())), preferred_element_type=jnp.float32
    )
    for j in range(per):
        out_ref[step * per + j, 0] = dqueries[:, j * width : (j + 1) * width].astype(jnp.bfloat16)

    @pl.when(step == pl.num_programs(0) - 1)
    def _():
        for s in range(blocks):
            out_ref[s, 1] = (dkeys_ref[s * width : (s + 1) * width, :].T * factor).astype(jnp.bfloat16)
            out_ref[s, 2] = dvalues_ref[s * width : (s + 1) * width, :].T.astype(jnp.bfloat16)


def whole(shape):
    return pl.BlockSpec(shape, lambda i: (0,) * len(shape))


def probs_call(heads):
    count, _, dims, width = heads.shape
    length = count * width
    block = min(BLOCK, length)
    return pl.pallas_call(
        probs_kernel,
        out_shape=jax.ShapeDtypeStruct((length, length), jnp.bfloat16),
        grid=(length // block,),
        in_specs=[whole(heads.shape)],
        out_specs=pl.BlockSpec((length, block), lambda i: (0, i)),
        scratch_shapes=[pltpu.VMEM((length, dims), jnp.bfloat16)],
        compiler_params=pltpu.CompilerParams(vmem_limit_bytes=48 * 2**20),
        cost_estimate=pl.CostEstimate(
            flops=2 * length * length * 256, transcendentals=length * length, bytes_accessed=2 * length * length
        ),
        name="probs",
    )(heads)


def grads_call(heads, grad, probs):
    count, _, dims, width = heads.shape
    length = count * width
    block = min(BLOCK, length)
    return pl.pallas_call(
        grads_kernel,
        out_shape=jax.ShapeDtypeStruct(heads.shape, jnp.bfloat16),
        grid=(length // block,),
        in_specs=[whole(heads.shape), whole(grad.shape), pl.BlockSpec((length, block), lambda i: (0, i))],
        out_specs=whole(heads.shape),
        scratch_shapes=[
            pltpu.VMEM((dims, length), jnp.bfloat16),
            pltpu.VMEM((length, dims), jnp.bfloat16),
            pltpu.VMEM((length // block, dims, block), jnp.bfloat16),
            pltpu.VMEM((length, dims), jnp.float32),
            pltpu.VMEM((length, dims), jnp.float32),
        ],
        compiler_params=pltpu.CompilerParams(vmem_limit_bytes=48 * 2**20),
        cost_estimate=pl.CostEstimate(
            flops=8 * length * length * 256, transcendentals=0, bytes_accessed=2 * length * length
        ),
        name="grads",
    )(heads, grad, probs)


def term_kernel(core_ref, dout_ref, out_in_ref, kept_ref, sent_ref, *, factor):
    half = out_in_ref.shape[1] // 2
    turned = dout_ref[...].T
    for side in range(2):
        product = lax.dot_general(
            turned,
            out_in_ref[:, side * half : (side + 1) * half],
            (((1,), (0,)), ((), ())),
            preferred_element_type=jnp.float32,
        )
        rounded = (product * factor).astype(jnp.bfloat16)
        if side == 0:
            kept_ref[:, half:] = jnp.zeros_like(kept_ref[:, half:])
            sent_ref[:, half:] = jnp.zeros_like(sent_ref[:, half:])

        @pl.when(core_ref[0] == side)
        def _():
            kept_ref[:, :half] = rounded

        @pl.when(core_ref[0] != side)
        def _():
            sent_ref[:, :half] = rounded


def term_call(core, dout, attn_out, factor):
    tokens, width = dout.shape
    kind = jax.ShapeDtypeStruct((width, pl.cdiv(width // 2, LANES) * LANES), jnp.bfloat16)
    vmem = pl.BlockSpec(memory_space=pltpu.VMEM)
    return pl.pallas_call(
        lambda *refs: term_kernel(*refs, factor=factor),
        out_shape=(kind, kind),
        in_specs=[pl.BlockSpec(memory_space=pltpu.SMEM), vmem, vmem],
        out_specs=(vmem, vmem),
        compiler_params=pltpu.CompilerParams(vmem_limit_bytes=32 * 2**20),
        cost_estimate=pl.CostEstimate(
            flops=2 * width * width * 256, transcendentals=0, bytes_accessed=2 * width * width
        ),
        name="term",
    )(core, dout, attn_out)


def project_kernel(core_ref, own_ref, other_ref, dout_ref, near_ref, out_ref, rows_ref):
    blocks = out_ref.shape[0] * 2
    width = dout_ref.shape[0]
    count = rows_ref.shape[2]
    tokens = jnp.concatenate([dout_ref[...], near_ref[...]], axis=0)
    for source, flip in ((own_ref, 0), (other_ref, 1)):
        product = lax.dot_general(
            source[...], tokens, (((1,), (1,)), ((), ())), preferred_element_type=jnp.float32
        )
        for parity in range(2):

            @pl.when(core_ref[0] == parity ^ flip)
            def _():
                for b in range(blocks):
                    start = ((b % 2) * 2 + parity) * SHARE
                    for side in range(2):
                        rows_ref[b // 2, side, start : start + SHARE, :] = product[
                            b * SHARE : (b + 1) * SHARE, side * width : (side + 1) * width
                        ]

    stride = out_ref.shape[1] // 2
    for side in range(2):
        out_ref[:, side * stride : side * stride + count, :] = rows_ref[:, side].astype(jnp.bfloat16)
        out_ref[:, side * stride + count : (side + 1) * stride, :] = jnp.zeros(
            (blocks // 2, stride - count, width), jnp.bfloat16
        )


def project_call(core, own, other, dout, near, heads):
    tokens, width = dout.shape
    count = 2 * own.shape[0] // heads
    shape = (heads, 2 * (pl.cdiv(count, 8) * 8), tokens)
    vmem = pl.BlockSpec(memory_space=pltpu.VMEM)
    return pl.pallas_call(
        project_kernel,
        out_shape=jax.ShapeDtypeStruct(shape, jnp.bfloat16),
        in_specs=[pl.BlockSpec(memory_space=pltpu.SMEM), vmem, vmem, vmem, vmem],
        out_specs=vmem,
        scratch_shapes=[pltpu.VMEM((heads, 2, count, tokens), jnp.float32)],
        compiler_params=pltpu.CompilerParams(vmem_limit_bytes=32 * 2**20),
        cost_estimate=pl.CostEstimate(
            flops=4 * width * width * tokens, transcendentals=0, bytes_accessed=4 * width * width
        ),
        name="project",
    )(core, own, other, dout, near)


SEQ = ("zl", "y")
ROWS = ("zh", "x")
DP = ("zh", "x", "c")
SHARE = 9
LANES = 128
SWAP = [(0, 1), (1, 0)]


def exchange(array, axes):
    return lax.all_to_all(array, axes, 0, 0, tiled=True)


def per_device(qkv, attn_out, dout, w_master, mom1, mom2, grad_prev):
    tokens, _, width = qkv.shape
    seq_count = lax.axis_size(SEQ)
    row_count = lax.axis_size(ROWS)
    rows, cols = w_master.shape
    core = lax.axis_index("c")
    core_id = core[None].astype(jnp.int32)

    moment_one = BETA_ONE * mom1 + (1.0 - BETA_ONE) * grad_prev
    moment_two = BETA_TWO * mom2 + (1.0 - BETA_TWO) * grad_prev * grad_prev
    weight_new = w_master - LEARN_RATE * (moment_one / CORRECT_ONE) / (
        jnp.sqrt(moment_two / CORRECT_TWO) + ADAM_EPS
    )
    weight_half = weight_new.astype(jnp.bfloat16)

    by_head = jnp.transpose(qkv.reshape(tokens, 3, seq_count, HD), (2, 1, 3, 0)).reshape(seq_count, 3 * HD, tokens)
    size = SHARE * cols
    flat = jnp.pad(weight_half.reshape(2, size), ((0, 0), (0, 8 * LANES - size))).reshape(2, 1, 8, LANES)
    flat = jnp.broadcast_to(flat, (2, seq_count // 2, 8, LANES)).reshape(seq_count, 8, LANES)
    packed = jnp.concatenate([by_head, flat], axis=1)
    packed, dout, attn_out = lax.optimization_barrier((packed, dout, attn_out))
    near = lax.ppermute(dout, "zl", SWAP)
    arrived = exchange(packed, SEQ)
    heads_qkv = arrived[:, : 3 * HD].reshape(seq_count, 3, HD, tokens)
    columns = arrived[:, 3 * HD :].reshape(seq_count, 8 * LANES)[:, :size].reshape(seq_count, SHARE, cols)

    factor = float(tokens * seq_count * lax.axis_size(DP)) ** (-0.5)
    kept, sent = term_call(core_id, dout, attn_out, factor)
    sent = lax.ppermute(sent, "c", SWAP)
    pair = (kept.astype(jnp.float32) + sent.astype(jnp.float32)).astype(jnp.bfloat16)

    row_block = jnp.transpose(columns, (1, 0, 2)).reshape(SHARE * width // LANES, LANES)
    row_block, pair, near = lax.optimization_barrier((row_block, pair, near))
    own = exchange(jnp.broadcast_to(row_block[None], (row_count,) + row_block.shape), ROWS)
    probs = probs_call(heads_qkv)
    own, probs = lax.optimization_barrier((own, probs))
    own = own.reshape(row_count * SHARE, width)
    other = lax.ppermute(own, "c", SWAP)
    grad_rows = project_call(core_id, own, other, dout, near, seq_count)
    heads_grad = exchange(grad_rows, SEQ)

    clip = lax.psum_scatter(pair, SEQ, scatter_dimension=0, tiled=True)
    clip, heads_grad = lax.optimization_barrier((clip, heads_grad))
    line, across = lax.axis_size("x"), lax.axis_size("zh")
    pieces = jnp.transpose(clip[:, : width // 2].T.reshape(across, line, rows * cols), (1, 0, 2))
    pieces = jnp.sum(exchange(pieces, "x").astype(jnp.float32), axis=0)
    grad_new = jnp.zeros((rows * cols,), jnp.float32)
    for turn in range(across):
        moves = [
            ((z * line + x) * 2 + c, (c * across + (z + turn) % across) * line + x)
            for z in range(across)
            for x in range(line)
            for c in range(2)
        ]
        piece = lax.dynamic_slice_in_dim(pieces, (lax.axis_index("zh") + turn) % across, 1, 0)[0]
        grad_new = grad_new + lax.ppermute(piece, DP, moves)
    grad_new = grad_new.reshape(rows, cols)

    local = grads_call(heads_qkv, heads_grad, probs)
    back = exchange(local, SEQ)
    dqkv = jnp.transpose(back, (3, 1, 0, 2)).reshape(tokens, 3, width)
    return (dqkv, grad_new, weight_new, moment_one, moment_two)


def solution(mesh):
    fine = Mesh(mesh.devices.reshape(4, 8, 2, 2, 8), ("zh", "x", "c", "zl", "y"))
    rows = P(DP + SEQ)
    square = P(DP, SEQ)
    return jax.shard_map(
        per_device,
        mesh=fine,
        in_specs=(rows, rows, rows, square, square, square, square),
        out_specs=(rows, square, square, square, square),
        check_vma=False,
    )
```

time: 560 us -> 214 us (0.38)
  the two profiles are of different devices: /device:TPU:1 before, /device:TPU:21 now
where the time goes in v1:
time: 214 us; the launch traced here: 213 us
  starting transfers between devices  88.8 us (41%)
  waiting for transfers between devices  47.6 us (22%)
  Pallas kernels  29.8 us (14%)
  blocking collectives  16.6 us (8%)
  between operations  14.3 us (7%)
  local copies, waits for them, and re-layouts  10.2 us (5%)
  other arithmetic  5.36 us (3%)
    all_to_all x4, starting transfers between devices, exchange(): return lax.all_to_all(array, axes, 0, 0, tiled=True)  41.7 us
    ppermute x4, starting transfers between devices, per_device(): grad_new = grad_new + lax.ppermute(piece, DP, moves)  36.4 us
    all_to_all x4, waiting for transfers between devices, exchange(): return lax.all_to_all(array, axes, 0, 0, tiled=True)  25.7 us
    all_to_all x1, blocking collectives, exchange(): return lax.all_to_all(array, axes, 0, 0, tiled=True)  16.6 us
    pallas_call x1, Pallas kernels, grads_call(): pl.pallas_call(grads_kernel, out_shape=jax.ShapeDtypeStruct(heads.shape,...  16 us
    optimization_barrier x1, waiting for transfers between devices, per_device(): clip, heads_grad = lax.optimization_barrier((clip, heads_grad))  13.1 us
    pallas_call x1, Pallas kernels, probs_call(): pl.pallas_call(probs_kernel, out_shape=jax.ShapeDtypeStruct((length, leng...  10.8 us
    ppermute x4, waiting for transfers between devices, per_device(): grad_new = grad_new + lax.ppermute(piece, DP, moves)  7 us
  transfers between devices with their start and end apart: 12, of which 5 were waited for; matrix products, arithmetic and copies ran while one was open for 4% of the time, Pallas kernels for 13%

profile of v1, /device:TPU:21, one launch (start us, length us, event | category | flops | bytes accessed | tf_op | source)
XLA Modules:
  0.0 212.6 jit_solution(11105892459480383704)
XLA Ops:
  7.2 1.4 fusion.1
  8.6 0.1 reshape.51
  8.7 1.8 copy.24
  10.5 0.0 copy-start
  10.5 0.0 copy-start.1
  10.5 0.1 copy.25
  10.6 1.0 pad_maximum_fusion
  11.6 1.8 term.1
  13.5 2.6 %collective-permute-start = (bf16[1152,640]{1,0:T(8,128)(2,1)S(1)}, bf16[1152,640]{1,0:T(8,128)(2,1)}, u32[]{:S(2)}, u32[]{:S(2)}) collective-permute-start(bf16[1152,640]{1,0:T(8,128)(2,1)S(1)} %get-tuple-element.21), channel_id=1, source_target_pairs={{0,16},{16,0},{1,17},{17,1},{2,18},{18,2},{3,19},{19,3},{4,20},{20... | collective-permute-start | bytes 4423688 | tf_op jit(solution)/shard_map/ppermute | solution.py:289
  16.0 10.1 %all-to-all-start = ((bf16[16,224,128]{2,1,0:T(8,128)(2,1)}), bf16[16,224,128]{2,1,0:T(8,128)(2,1)}, u32[]{:S(2)}, u32[]{:S(2)}) async-start(bf16[16,224,128]{2,1,0:T(8,128)(2,1)} %pad_maximum_fusion), calls=%async_computation | async-start | bytes 1835008 | tf_op jit(solution)/shard_map/all_to_all | solution.py:258
  26.1 0.0 reduce-scatter.5.cloned.1.call-start
  26.2 3.1 %collective-permute-start.1 = (bf16[128,1152]{1,0:T(8,128)(2,1)S(1)}, bf16[128,1152]{1,0:T(8,128)(2,1)S(1)}, u32[]{:S(2)}, u32[]{:S(2)}) collective-permute-start(bf16[128,1152]{1,0:T(8,128)(2,1)S(1)} %copy-done.1), channel_id=1, source_target_pairs={{0,8},{8,0},{1,9},{9,1},{2,10},{10,2},{3,11},{11,3},{4,12},{12,4},... | collective-permute-start | bytes 884744 | tf_op jit(solution)/shard_map/ppermute | solution.py:282
  29.3 0.0 collective-permute-done
  29.3 2.9 %add_convert_fusion = bf16[1152,640]{1,0:T(8,128)(2,1)} fusion(bf16[1152,640]{1,0:T(8,128)(2,1)} %collective-permute-done, bf16[1152,640]{1,0:T(8,128)(2,1)S(1)} %get-tuple-element.20), kind=kLoop, calls=%fused_computation | loop fusion | flops 2949120 | bytes 4423680 | tf_op jit(solution)/shard_map/convert_element_type | solution.py:290
  32.2 16.7 %all-to-all-done = bf16[16,224,128]{2,1,0:T(8,128)(2,1)} async-done(((bf16[16,224,128]{2,1,0:T(8,128)(2,1)}), bf16[16,224,128]{2,1,0:T(8,128)(2,1)}, u32[]{:S(2)}, u32[]{:S(2)}) %all-to-all-start) | async-done | bytes 917536 | tf_op jit(solution)/shard_map/all_to_all | solution.py:258
  48.9 0.8 slice.17
  49.7 0.1 reshape.55
  49.8 0.1 reshape.56
  50.0 0.0 collective-permute-done.1.near_ref
  50.0 0.0 reduce-scatter.5.cloned.1.call-update
  50.0 1.0 broadcast_in_dim.19
  51.0 19.9 %all-to-all-start.1 = ((bf16[32,81,128]{2,1,0:T(8,128)(2,1)}), bf16[32,81,128]{2,1,0:T(8,128)(2,1)S(1)}, u32[]{:S(2)}, u32[]{:S(2)}) async-start(bf16[32,81,128]{2,1,0:T(8,128)(2,1)} %broadcast_in_dim.19), calls=%async_computation.1 | async-start | bytes 1441792 | tf_op jit(solution)/shard_map/all_to_all | solution.py:258
  70.8 1.2 slice.16
  72.1 10.8 %probs.1.probs_ref = bf16[2048,2048]{1,0:T(8,128)(2,1)} custom-call(bf16[16,3,72,128]{3,2,1,0:T(8,128)(2,1)S(1)} %bitcast.23), custom_call_target="tpu_custom_call" | custom-call | flops 2147483648 | bytes 8388608 | tf_op jit(solution)/shard_map/probs/pallas_call | solution.py:121
  82.9 9.0 %all-to-all-done.1 = bf16[32,81,128]{2,1,0:T(8,128)(2,1)S(1)} async-done(((bf16[32,81,128]{2,1,0:T(8,128)(2,1)}), bf16[32,81,128]{2,1,0:T(8,128)(2,1)S(1)}, u32[]{:S(2)}, u32[]{:S(2)}) %all-to-all-start.1) | async-done | bytes 663584 | tf_op jit(solution)/shard_map/all_to_all | solution.py:258
  91.9 0.8 reshape.57.own_ref
  92.7 4.9 %collective-permute-start.2 = (bf16[288,1152]{1,0:T(8,128)(2,1)S(1)}, bf16[288,1152]{1,0:T(8,128)(2,1)S(1)}, u32[]{:S(2)}, u32[]{:S(2)}) collective-permute-start(bf16[288,1152]{1,0:T(8,128)(2,1)S(1)} %reshape.57.own_ref), channel_id=1, source_target_pairs={{0,16},{16,0},{1,17},{17,1},{2,18},{18,2},{3,19},{19,3},{4,20},{20... | collective-permute-start | bytes 1990664 | tf_op jit(solution)/shard_map/ppermute | solution.py:298
  97.6 1.7 collective-permute-done.2.other_ref
  99.3 1.2 project.1
  100.5 16.6 %all_to_all.25.grad_ref = bf16[16,80,128]{2,1,0:T(8,128)(2,1)S(1)} all-to-all(bf16[16,80,128]{2,1,0:T(8,128)(2,1)S(1)} %project.1), channel_id=1, replica_groups=mesh['zh'=4,'x'=8,'c'=2,'zl'=2,'y'=8] {'zl','y'}, dimensions={0} | all-to-all | bytes 655360 | tf_op jit(solution)/shard_map/all_to_all | solution.py:258
  117.2 13.1 %reduce-scatter.5.cloned.1.call-done = bf16[72,640]{1,0:T(8,128)(2,1)} async-done(((bf16[1152,640]{1,0:T(8,128)(2,1)}), bf16[72,640]{1,0:T(8,128)(2,1)}) %reduce-scatter.5.cloned.1.call-update) | async-done | bytes 92176 | tf_op jit(solution)/shard_map/optimization_barrier | solution.py:303
  130.3 0.9 slice_bitcast_fusion
  131.2 0.1 copy.28
  131.3 0.2 reshape.59
  131.5 0.7 copy.29
  132.1 5.9 %all-to-all-start.4 = ((bf16[8,4,1296]{2,1,0:T(4,128)(2,1)}), bf16[8,4,1296]{2,1,0:T(4,128)(2,1)S(1)}, u32[]{:S(2)}, u32[]{:S(2)}) async-start(bf16[8,4,1296]{2,1,0:T(4,128)(2,1)} %copy.29), calls=%async_computation.4 | async-start | bytes 180224 | tf_op jit(solution)/shard_map/all_to_all | solution.py:258
  138.0 16.0 %grads.1 = bf16[16,3,72,128]{3,2,1,0:T(8,128)(2,1)} custom-call(bf16[16,3,72,128]{3,2,1,0:T(8,128)(2,1)S(1)} %bitcast.24, bf16[16,80,128]{2,1,0:T(8,128)(2,1)S(1)} %all_to_all.25.grad_ref, bf16[2048,2048]{1,0:T(8,128)(2,1)} %probs.1.probs_ref), custom_call_target="tpu_custom_call" | custom-call | flops 8589934592 | bytes 8388608 | tf_op jit(solution)/shard_map/grads/pallas_call | solution.py:140
  154.0 5.8 %all-to-all-start.3 = ((bf16[16,3,72,128]{3,2,1,0:T(8,128)(2,1)}), bf16[16,3,72,128]{3,2,1,0:T(8,128)(2,1)S(1)}, u32[]{:S(2)}, u32[]{:S(2)}) async-start(bf16[16,3,72,128]{3,2,1,0:T(8,128)(2,1)} %grads.1), calls=%async_computation.3 | async-start | bytes 1769472 | tf_op jit(solution)/shard_map/all_to_all | solution.py:258
  159.8 0.1 convert_reduce_fusion
  159.9 0.1 dynamic-slice_reduce_fusion.2
  160.0 21.1 %collective-permute-start.6 = (f32[1296]{0:T(1024)S(1)}, f32[1296]{0:T(1024)S(1)}, u32[]{:S(2)}, u32[]{:S(2)}) collective-permute-start(f32[1296]{0:T(1024)S(1)} %get-tuple-element.45), channel_id=1, source_target_pairs={{0,384},{16,896},{32,400},{48,912},{64,416},{80,928},{96,432},{112... | collective-permute-start | bytes 15560 | tf_op jit(solution)/shard_map/ppermute | solution.py:316
  181.1 1.9 collective-permute-start.5
  183.0 9.3 %collective-permute-start.3 = (f32[1296]{0:T(1024)S(1)}, f32[1296]{0:T(1024)S(1)}, u32[]{:S(2)}, u32[]{:S(2)}) collective-permute-start(f32[1296]{0:T(1024)S(1)} %get-tuple-element.47), channel_id=1, source_target_pairs={{0,0},{16,512},{32,16},{48,528},{64,32},{80,544},{96,48},{112,560}... | collective-permute-start | bytes 15560 | tf_op jit(solution)/shard_map/ppermute | solution.py:316
  192.4 4.0 %collective-permute-start.4 = (f32[1296]{0:T(1024)S(1)}, f32[1296]{0:T(1024)S(1)}, u32[]{:S(2)}, u32[]{:S(2)}) collective-permute-start(f32[1296]{0:T(1024)S(1)} %get-tuple-element.44), channel_id=1, source_target_pairs={{0,128},{16,640},{32,144},{48,656},{64,160},{80,672},{96,176},{112... | collective-permute-start | bytes 15560 | tf_op jit(solution)/shard_map/ppermute | solution.py:316
  196.5 7.0 %collective-permute-done.4 = f32[1296]{0:T(1024)S(1)} collective-permute-done((f32[1296]{0:T(1024)S(1)}, f32[1296]{0:T(1024)S(1)}, u32[]{:S(2)}, u32[]{:S(2)}) %collective-permute-start.4) | collective-permute-done | bytes 5216 | tf_op jit(solution)/shard_map/ppermute | solution.py:316
  203.5 0.7 reshape.60
  204.2 0.1 copy.27
  204.2 1.5 copy.30
  (14 shorter events, 0.1 us)
Async XLA Ops:
  10.5 1.1 copy-start
  10.5 1.1 copy-start.1
  13.5 15.8 %collective-permute-start = (bf16[1152,640]{1,0:T(8,128)(2,1)S(1)}, bf16[1152,640]{1,0:T(8,128)(2,1)}, u32[]{:S(2)}, u32[]{:S(2)}) collective-permute-start(bf16[1152,640]{1,0:T(8,128)(2,1)S(1)} %get-tuple-element.21), channel_id=1, source_target_pairs={{0,16},{16,0},{1,17},{17,1},{2,18},{18,2},{3,19},{19,3},{4,20},{20... | collective-permute-start | bytes 4423688 | tf_op jit(solution)/shard_map/ppermute | solution.py:289
  16.0 32.9 %all-to-all-start = ((bf16[16,224,128]{2,1,0:T(8,128)(2,1)}), bf16[16,224,128]{2,1,0:T(8,128)(2,1)}, u32[]{:S(2)}, u32[]{:S(2)}) async-start(bf16[16,224,128]{2,1,0:T(8,128)(2,1)} %pad_maximum_fusion), calls=%async_computation | async-start | bytes 1835008 | tf_op jit(solution)/shard_map/all_to_all | solution.py:258
  26.1 104.2 %reduce-scatter.5.cloned.1.call-start = ((), (), s32[]{:S(2)}) async-start(), calls=%async_computation.6 | async-start | bytes 1566720
  26.2 23.8 %collective-permute-start.1 = (bf16[128,1152]{1,0:T(8,128)(2,1)S(1)}, bf16[128,1152]{1,0:T(8,128)(2,1)S(1)}, u32[]{:S(2)}, u32[]{:S(2)}) collective-permute-start(bf16[128,1152]{1,0:T(8,128)(2,1)S(1)} %copy-done.1), channel_id=1, source_target_pairs={{0,8},{8,0},{1,9},{9,1},{2,10},{10,2},{3,11},{11,3},{4,12},{12,4},... | collective-permute-start | bytes 884744 | tf_op jit(solution)/shard_map/ppermute | solution.py:282
  51.0 40.9 %all-to-all-start.1 = ((bf16[32,81,128]{2,1,0:T(8,128)(2,1)}), bf16[32,81,128]{2,1,0:T(8,128)(2,1)S(1)}, u32[]{:S(2)}, u32[]{:S(2)}) async-start(bf16[32,81,128]{2,1,0:T(8,128)(2,1)} %broadcast_in_dim.19), calls=%async_computation.1 | async-start | bytes 1441792 | tf_op jit(solution)/shard_map/all_to_all | solution.py:258
  92.7 6.7 %collective-permute-start.2 = (bf16[288,1152]{1,0:T(8,128)(2,1)S(1)}, bf16[288,1152]{1,0:T(8,128)(2,1)S(1)}, u32[]{:S(2)}, u32[]{:S(2)}) collective-permute-start(bf16[288,1152]{1,0:T(8,128)(2,1)S(1)} %reshape.57.own_ref), channel_id=1, source_target_pairs={{0,16},{16,0},{1,17},{17,1},{2,18},{18,2},{3,19},{19,3},{4,20},{20... | collective-permute-start | bytes 1990664 | tf_op jit(solution)/shard_map/ppermute | solution.py:298
  132.1 21.9 %all-to-all-start.4 = ((bf16[8,4,1296]{2,1,0:T(4,128)(2,1)}), bf16[8,4,1296]{2,1,0:T(4,128)(2,1)S(1)}, u32[]{:S(2)}, u32[]{:S(2)}) async-start(bf16[8,4,1296]{2,1,0:T(4,128)(2,1)} %copy.29), calls=%async_computation.4 | async-start | bytes 180224 | tf_op jit(solution)/shard_map/all_to_all | solution.py:258
  154.0 50.1 %all-to-all-start.3 = ((bf16[16,3,72,128]{3,2,1,0:T(8,128)(2,1)}), bf16[16,3,72,128]{3,2,1,0:T(8,128)(2,1)S(1)}, u32[]{:S(2)}, u32[]{:S(2)}) async-start(bf16[16,3,72,128]{3,2,1,0:T(8,128)(2,1)} %grads.1), calls=%async_computation.3 | async-start | bytes 1769472 | tf_op jit(solution)/shard_map/all_to_all | solution.py:258
  160.0 36.5 %collective-permute-start.6 = (f32[1296]{0:T(1024)S(1)}, f32[1296]{0:T(1024)S(1)}, u32[]{:S(2)}, u32[]{:S(2)}) collective-permute-start(f32[1296]{0:T(1024)S(1)} %get-tuple-element.45), channel_id=1, source_target_pairs={{0,384},{16,896},{32,400},{48,912},{64,416},{80,928},{96,432},{112... | collective-permute-start | bytes 15560 | tf_op jit(solution)/shard_map/ppermute | solution.py:316
  181.1 15.3 %collective-permute-start.5 = (f32[1296]{0:T(1024)S(1)}, f32[1296]{0:T(1024)S(1)}, u32[]{:S(2)}, u32[]{:S(2)}) collective-permute-start(f32[1296]{0:T(1024)S(1)} %get-tuple-element.46), channel_id=1, source_target_pairs={{0,256},{16,768},{32,272},{48,784},{64,288},{80,800},{96,304},{112... | collective-permute-start | bytes 15560 | tf_op jit(solution)/shard_map/ppermute | solution.py:316
  183.0 13.4 %collective-permute-start.3 = (f32[1296]{0:T(1024)S(1)}, f32[1296]{0:T(1024)S(1)}, u32[]{:S(2)}, u32[]{:S(2)}) collective-permute-start(f32[1296]{0:T(1024)S(1)} %get-tuple-element.47), channel_id=1, source_target_pairs={{0,0},{16,512},{32,16},{48,528},{64,32},{80,544},{96,48},{112,560}... | collective-permute-start | bytes 15560 | tf_op jit(solution)/shard_map/ppermute | solution.py:316
  192.4 11.1 %collective-permute-start.4 = (f32[1296]{0:T(1024)S(1)}, f32[1296]{0:T(1024)S(1)}, u32[]{:S(2)}, u32[]{:S(2)}) collective-permute-start(f32[1296]{0:T(1024)S(1)} %get-tuple-element.44), channel_id=1, source_target_pairs={{0,128},{16,640},{32,144},{48,656},{64,160},{80,672},{96,176},{112... | collective-permute-start | bytes 15560 | tf_op jit(solution)/shard_map/ppermute | solution.py:316
Sparse Core Ops, SparseCore 0:
  50.1 80.1 reduce-scatter.4

commit v2 on v1

--- a/solution.py
+++ b/solution.py
@@ -1,3 +1,5 @@
+import math
+
 import jax
 import jax.numpy as jnp
 from jax import lax
@@ -246,9 +248,70 @@
     )(core, own, other, dout, near)
 
 
+def pick_kernel(place_ref, heads_ref, near_ref, *out_refs):
+    count = len(out_refs)
+    for turn in range(count):
+        target = (place_ref[1] + turn) % count
+        out_refs[turn][0] = heads_ref[place_ref[0] * count + target]
+        out_refs[turn][1] = near_ref[target]
+
+
+def place_kernel(place_ref, *refs):
+    in_refs, out_ref = refs[:-1], refs[-1]
+    count = len(in_refs)
+    for turn in range(count):
+        origin = (place_ref[1] + count - turn) % count
+        out_ref[place_ref[0] * count + origin] = in_refs[turn][0]
+        out_ref[(1 - place_ref[0]) * count + origin] = in_refs[turn][1]
+
+
+def arrange_kernel(place_ref, clip_ref, *refs):
+    out_refs, blocks_ref = refs[:-1], refs[-1]
+    line, across, rows = blocks_ref.shape[0], blocks_ref.shape[1], ROWS_DEV
+    cols = clip_ref.shape[1]
+    total = clip_ref[0].astype(jnp.float32)
+    for s in range(1, clip_ref.shape[0]):
+        total = total + clip_ref[s].astype(jnp.float32)
+    turned = total.T
+    blocks_ref[...] = jnp.zeros_like(blocks_ref)
+    for z in range(across):
+        for x in range(line):
+            start = (z * line + x) * rows
+            blocks_ref[x, z, :rows, :cols] = turned[start : start + rows]
+    for turn in range(line):
+        out_refs[turn][...] = blocks_ref[(place_ref[2] + turn) % line]
+
+
+def gather_kernel(place_ref, *refs):
+    total_ref, count = refs[-1], refs[-1].shape[0]
+    in_refs, out_refs = refs[: -1 - count], refs[-1 - count : -1]
+    total = in_refs[0][...]
+    for ref in in_refs[1:]:
+        total = total + ref[...]
+    total_ref[...] = total
+    for turn in range(count):
+        out_refs[turn][...] = total_ref[(place_ref[3] + turn) % count]
+
+
+def moved_call(kernel, name, place, operands, out_shape, scratch=()):
+    vmem = pl.BlockSpec(memory_space=pltpu.VMEM)
+    size = sum(operand.size for operand in operands)
+    return pl.pallas_call(
+        kernel,
+        out_shape=out_shape,
+        in_specs=[pl.BlockSpec(memory_space=pltpu.SMEM)] + [vmem] * len(operands),
+        out_specs=jax.tree.map(lambda leaf: vmem, out_shape),
+        scratch_shapes=scratch,
+        compiler_params=pltpu.CompilerParams(vmem_limit_bytes=16 * 2**20),
+        cost_estimate=pl.CostEstimate(flops=0, transcendentals=0, bytes_accessed=0 if scratch else 4 * size),
+        name=name,
+    )(place, *operands)
+
+
 SEQ = ("zl", "y")
 ROWS = ("zh", "x")
 DP = ("zh", "x", "c")
+ROWS_DEV = 18
 SHARE = 9
 LANES = 128
 SWAP = [(0, 1), (1, 0)]
@@ -256,15 +319,21 @@
 
 def exchange(array, axes):
     return lax.all_to_all(array, axes, 0, 0, tiled=True)
+
+
+def at(array, index):
+    return lax.dynamic_index_in_dim(array, index, 0, keepdims=False)
 
 
 def per_device(qkv, attn_out, dout, w_master, mom1, mom2, grad_prev):
     tokens, _, width = qkv.shape
     seq_count = lax.axis_size(SEQ)
     row_count = lax.axis_size(ROWS)
+    ring = lax.axis_size("y")
     rows, cols = w_master.shape
-    core = lax.axis_index("c")
+    core, side, step = lax.axis_index("c"), lax.axis_index("zl"), lax.axis_index("y")
     core_id = core[None].astype(jnp.int32)
+    place = jnp.stack([side, step, lax.axis_index("x"), lax.axis_index("zh")]).astype(jnp.int32)
 
     moment_one = BETA_ONE * mom1 + (1.0 - BETA_ONE) * grad_prev
     moment_two = BETA_TWO * mom2 + (1.0 - BETA_TWO) * grad_prev * grad_prev
@@ -273,38 +342,60 @@
     )
     weight_half = weight_new.astype(jnp.bfloat16)
 
-    by_head = jnp.transpose(qkv.reshape(tokens, 3, seq_count, HD), (2, 1, 3, 0)).reshape(seq_count, 3 * HD, tokens)
     size = SHARE * cols
     flat = jnp.pad(weight_half.reshape(2, size), ((0, 0), (0, 8 * LANES - size))).reshape(2, 1, 8, LANES)
     flat = jnp.broadcast_to(flat, (2, seq_count // 2, 8, LANES)).reshape(seq_count, 8, LANES)
-    packed = jnp.concatenate([by_head, flat], axis=1)
-    packed, dout, attn_out = lax.optimization_barrier((packed, dout, attn_out))
+    flat, qkv = lax.optimization_barrier((flat, qkv))
+    columns = exchange(flat, SEQ).reshape(seq_count, 8 * LANES)[:, :size].reshape(seq_count, SHARE, cols)
+
+    by_head = jnp.transpose(qkv.reshape(tokens, 3, seq_count, HD), (2, 1, 3, 0)).reshape(seq_count, 3 * HD, tokens)
+    passed = lax.ppermute(at(by_head.reshape(2, ring, 3 * HD, tokens), 1 - side), "zl", SWAP)
+    pair_of = jax.ShapeDtypeStruct((2, 3 * HD, tokens), jnp.bfloat16)
+    turns = list(moved_call(pick_kernel, "pick", place, (by_head, passed), (pair_of,) * ring))
+
+    lane = math.gcd(SHARE * width, LANES)
+    row_block = jnp.transpose(columns, (1, 0, 2)).reshape(SHARE * width // lane, lane)
+    row_block, turns, place = lax.optimization_barrier((row_block, turns, place))
+    row_block, dout, attn_out = lax.optimization_barrier((row_block, dout, attn_out))
     near = lax.ppermute(dout, "zl", SWAP)
-    arrived = exchange(packed, SEQ)
-    heads_qkv = arrived[:, : 3 * HD].reshape(seq_count, 3, HD, tokens)
-    columns = arrived[:, 3 * HD :].reshape(seq_count, 8 * LANES)[:, :size].reshape(seq_count, SHARE, cols)
+    own = exchange(jnp.broadcast_to(row_block[None], (row_count,) + row_block.shape), ROWS)
+    for turn in range(1, ring):
+        moves = [(i, (i + turn) % ring) for i in range(ring)]
+        turns[turn] = lax.ppermute(turns[turn], "y", moves)
+    heads = jax.ShapeDtypeStruct((seq_count, 3 * HD, tokens), jnp.bfloat16)
+    heads_qkv = moved_call(place_kernel, "place", place, tuple(turns), heads).reshape(seq_count, 3, HD, tokens)
+    own, heads_qkv, near = lax.optimization_barrier((own, heads_qkv, near))
+    own = own.reshape(row_count * SHARE, width)
+    other = lax.ppermute(own, "c", SWAP)
+    grad_rows = project_call(core_id, own, other, dout, near, seq_count)
+    grad_rows, heads_qkv = lax.optimization_barrier((grad_rows, heads_qkv))
+    heads_grad = exchange(grad_rows, SEQ)
+    probs = probs_call(heads_qkv)
 
     factor = float(tokens * seq_count * lax.axis_size(DP)) ** (-0.5)
     kept, sent = term_call(core_id, dout, attn_out, factor)
     sent = lax.ppermute(sent, "c", SWAP)
     pair = (kept.astype(jnp.float32) + sent.astype(jnp.float32)).astype(jnp.bfloat16)
-
-    row_block = jnp.transpose(columns, (1, 0, 2)).reshape(SHARE * width // LANES, LANES)
-    row_block, pair, near = lax.optimization_barrier((row_block, pair, near))
-    own = exchange(jnp.broadcast_to(row_block[None], (row_count,) + row_block.shape), ROWS)
-    probs = probs_call(heads_qkv)
-    own, probs = lax.optimization_barrier((own, probs))
-    own = own.reshape(row_count * SHARE, width)
-    other = lax.ppermute(own, "c", SWAP)
-    grad_rows = project_call(core_id, own, other, dout, near, seq_count)
-    heads_grad = exchange(grad_rows, SEQ)
-
-    clip = lax.psum_scatter(pair, SEQ, scatter_dimension=0, tiled=True)
-    clip, heads_grad = lax.optimization_barrier((clip, heads_grad))
+    pair = pair.reshape(2, width // 2, pair.shape[1])
+    sent = lax.ppermute(at(pair, 1 - side), "zl", SWAP)
+    quad = (at(pair, side).astype(jnp.float32) + sent.astype(jnp.float32)).astype(jnp.bfloat16)
+    quad, heads_grad, probs = lax.optimization_barrier((quad, heads_grad, probs))
+    clip = exchange(quad.reshape(ring, cols, quad.shape[1]), "y")
+    local = grads_call(heads_qkv, heads_grad, probs)
+    local, clip = lax.optimization_barrier((local, clip))
+
     line, across = lax.axis_size("x"), lax.axis_size("zh")
-    pieces = jnp.transpose(clip[:, : width // 2].T.reshape(across, line, rows * cols), (1, 0, 2))
-    pieces = jnp.sum(exchange(pieces, "x").astype(jnp.float32), axis=0)
-    grad_new = jnp.zeros((rows * cols,), jnp.float32)
+    kind = jax.ShapeDtypeStruct((across, 24, LANES), jnp.float32)
+    scratch = [pltpu.VMEM((line,) + kind.shape, jnp.float32)]
+    pieces = moved_call(arrange_kernel, "arrange", place, (clip,), (kind,) * line, scratch)
+    pieces = list(pieces)
+    for turn in range(1, line):
+        moves = [(i, (i + turn) % line) for i in range(line)]
+        pieces[turn] = lax.ppermute(pieces[turn], "x", moves)
+    block = jax.ShapeDtypeStruct(kind.shape[1:], jnp.float32)
+    scratch = [pltpu.VMEM(kind.shape, jnp.float32)]
+    pieces = moved_call(gather_kernel, "gather", place, tuple(pieces), (block,) * across, scratch)
+    grad_new = jnp.zeros((24, LANES), jnp.float32)
     for turn in range(across):
         moves = [
             ((z * line + x) * 2 + c, (c * across + (z + turn) % across) * line + x)
@@ -312,11 +403,9 @@
             for x in range(line)
             for c in range(2)
         ]
-        piece = lax.dynamic_slice_in_dim(pieces, (lax.axis_index("zh") + turn) % across, 1, 0)[0]
-        grad_new = grad_new + lax.ppermute(piece, DP, moves)
-    grad_new = grad_new.reshape(rows, cols)
-
-    local = grads_call(heads_qkv, heads_grad, probs)
+        grad_new = grad_new + lax.ppermute(pieces[turn], DP, moves)
+    grad_new = grad_new[:rows, :cols]
+
     back = exchange(local, SEQ)
     dqkv = jnp.transpose(back, (3, 1, 0, 2)).reshape(tokens, 3, width)
     return (dqkv, grad_new, weight_new, moment_one, moment_two)

time: 214 us -> 221 us (1.033)
  the two profiles are of different devices: /device:TPU:21 before, /device:TPU:277 now
where the time goes in v2:
time: 221 us; the launch traced here: 219 us
  starting transfers between devices  134 us (61%)
  Pallas kernels  34.3 us (16%)
  waiting for transfers between devices  33.4 us (15%)
  local copies, waits for them, and re-layouts  11.3 us (5%)
  other arithmetic  4.86 us (2%)
    all_to_all x5, starting transfers between devices, exchange(): return lax.all_to_all(array, axes, 0, 0, tiled=True)  42.2 us
    ppermute x7, starting transfers between devices, per_device(): pieces[turn] = lax.ppermute(pieces[turn], 'x', moves)  25 us
    ppermute x4, starting transfers between devices, per_device(): grad_new = grad_new + lax.ppermute(pieces[turn], DP, moves)  24.8 us
    ppermute x7, starting transfers between devices, per_device(): turns[turn] = lax.ppermute(turns[turn], 'y', moves)  24.3 us
    pallas_call x1, Pallas kernels, grads_call(): pl.pallas_call(grads_kernel, out_shape=jax.ShapeDtypeStruct(heads.shape,...  16 us
    pallas_call x1, Pallas kernels, probs_call(): pl.pallas_call(probs_kernel, out_shape=jax.ShapeDtypeStruct((length, leng...  10.8 us
    ppermute x4, waiting for transfers between devices, per_device(): grad_new = grad_new + lax.ppermute(pieces[turn], DP, moves)  10.6 us
    ppermute x7, waiting for transfers between devices, per_device(): turns[turn] = lax.ppermute(turns[turn], 'y', moves)  10.3 us
  transfers between devices with their start and end apart: 28, of which 9 were waited for; matrix products, arithmetic and copies ran while one was open for 3% of the time, Pallas kernels for 14%

profile of v2, /device:TPU:277, one launch (start us, length us, event | category | flops | bytes accessed | tf_op | source)
XLA Modules:
  0.0 219.5 jit_solution(15451055330141647359)
XLA Ops:
  0.6 1.4 fusion.2
  2.8 1.8 copy.18
  4.7 5.0 %collective-permute-start = (bf16[8,216,128]{2,1,0:T(8,128)(2,1)S(1)}, bf16[8,216,128]{2,1,0:T(8,128)(2,1)S(1)}, u32[]{:S(2)}, u32[]{:S(2)}) collective-permute-start(bf16[8,216,128]{2,1,0:T(8,128)(2,1)S(1)} %dynamic-slice_bitcast_fusion.1), channel_id=1, source_target_pairs={{0,8},{8,0},{1,9},{9,1},{2,10},{10,2},{3,11},{11,3},{4,12},{12,4},... | collective-permute-start | bytes 1327112 | tf_op jit(solution)/shard_map/ppermute | solution.py:352
  9.8 7.4 %all-to-all-start = ((bf16[16,8,128]{2,1,0:T(8,128)(2,1)}), bf16[16,8,128]{2,1,0:T(8,128)(2,1)S(1)}, u32[]{:S(2)}, u32[]{:S(2)}) async-start(bf16[16,8,128]{2,1,0:T(8,128)(2,1)} %bitcast.1), calls=%async_computation | async-start | bytes 65536 | tf_op jit(solution)/shard_map/all_to_all | solution.py:321
  17.2 6.3 %all-to-all-done = bf16[16,8,128]{2,1,0:T(8,128)(2,1)S(1)} async-done(((bf16[16,8,128]{2,1,0:T(8,128)(2,1)}), bf16[16,8,128]{2,1,0:T(8,128)(2,1)S(1)}, u32[]{:S(2)}, u32[]{:S(2)}) %all-to-all-start) | async-done | bytes 32800 | tf_op jit(solution)/shard_map/all_to_all | solution.py:321
  26.4 3.0 %term.1 = (bf16[1152,640]{1,0:T(8,128)(2,1)S(1)}, bf16[1152,640]{1,0:T(8,128)(2,1)}) custom-call(s32[1]{0:T(128)} %bitcast.core_ref.refs_0_, bf16[128,1152]{1,0:T(8,128)(2,1)S(1)} %copy-done.1, bf16[128,1152]{1,0:T(8,128)(2,1)S(1)} %copy-done), custom_call_target="tpu_custom_call" | custom-call | flops 679477248 | bytes 2654208 | tf_op jit(solution)/shard_map/term/pallas_call | solution.py:191
  29.3 4.4 %collective-permute-start.10 = (bf16[1152,640]{1,0:T(8,128)(2,1)}, bf16[1152,640]{1,0:T(8,128)(2,1)}, u32[]{:S(2)}, u32[]{:S(2)}) collective-permute-start(bf16[1152,640]{1,0:T(8,128)(2,1)} %get-tuple-element.80), channel_id=1, source_target_pairs={{0,16},{16,0},{1,17},{17,1},{2,18},{18,2},{3,19},{19,3},{4,20},{20... | collective-permute-start | bytes 4423688 | tf_op jit(solution)/shard_map/ppermute | solution.py:377
  33.8 1.0 broadcast_in_dim.19
  34.7 16.3 %all-to-all-start.1 = ((bf16[32,81,128]{2,1,0:T(8,128)(2,1)}), bf16[32,81,128]{2,1,0:T(8,128)(2,1)}, u32[]{:S(2)}, u32[]{:S(2)}) async-start(bf16[32,81,128]{2,1,0:T(8,128)(2,1)} %broadcast_in_dim.19), calls=%async_computation.1 | async-start | bytes 1441792 | tf_op jit(solution)/shard_map/all_to_all | solution.py:321
  51.0 2.4 %collective-permute-start.1 = (bf16[2,216,128]{2,1,0:T(8,128)(2,1)S(1)}, bf16[2,216,128]{2,1,0:T(8,128)(2,1)S(1)}, u32[]{:S(2)}, u32[]{:S(2)}) collective-permute-start(bf16[2,216,128]{2,1,0:T(8,128)(2,1)S(1)} %copy-done.9), channel_id=1, source_target_pairs={{0,1},{1,2},{2,3},{3,4},{4,5},{5,6},{6,7},{7,0},{8,9},{9,10},{10,1... | collective-permute-start | bytes 331784 | tf_op jit(solution)/shard_map/ppermute | solution.py:364
  53.4 2.2 %collective-permute-start.8 = (bf16[128,1152]{1,0:T(8,128)(2,1)S(1)}, bf16[128,1152]{1,0:T(8,128)(2,1)S(1)}, u32[]{:S(2)}, u32[]{:S(2)}) collective-permute-start(bf16[128,1152]{1,0:T(8,128)(2,1)S(1)} %copy-done.1), channel_id=1, source_target_pairs={{0,8},{8,0},{1,9},{9,1},{2,10},{10,2},{3,11},{11,3},{4,12},{12,4},... | collective-permute-start | bytes 884744 | tf_op jit(solution)/shard_map/ppermute | solution.py:360
  55.7 3.1 %collective-permute-start.2 = (bf16[2,216,128]{2,1,0:T(8,128)(2,1)S(1)}, bf16[2,216,128]{2,1,0:T(8,128)(2,1)S(1)}, u32[]{:S(2)}, u32[]{:S(2)}) collective-permute-start(bf16[2,216,128]{2,1,0:T(8,128)(2,1)S(1)} %copy-done.7), channel_id=1, source_target_pairs={{0,2},{1,3},{2,4},{3,5},{4,6},{5,7},{6,0},{7,1},{8,10},{9,11},{10,... | collective-permute-start | bytes 331784 | tf_op jit(solution)/shard_map/ppermute | solution.py:364
  58.8 4.0 %collective-permute-start.3 = (bf16[2,216,128]{2,1,0:T(8,128)(2,1)S(1)}, bf16[2,216,128]{2,1,0:T(8,128)(2,1)S(1)}, u32[]{:S(2)}, u32[]{:S(2)}) collective-permute-start(bf16[2,216,128]{2,1,0:T(8,128)(2,1)S(1)} %copy-done.5), channel_id=1, source_target_pairs={{0,3},{1,4},{2,5},{3,6},{4,7},{5,0},{6,1},{7,2},{8,11},{9,12},{10,... | collective-permute-start | bytes 331784 | tf_op jit(solution)/shard_map/ppermute | solution.py:364
  62.8 4.3 %collective-permute-start.4 = (bf16[2,216,128]{2,1,0:T(8,128)(2,1)S(1)}, bf16[2,216,128]{2,1,0:T(8,128)(2,1)S(1)}, u32[]{:S(2)}, u32[]{:S(2)}) collective-permute-start(bf16[2,216,128]{2,1,0:T(8,128)(2,1)S(1)} %get-tuple-element.69), channel_id=1, source_target_pairs={{0,4},{1,5},{2,6},{3,7},{4,0},{5,1},{6,2},{7,3},{8,12},{9,13},{10,... | collective-permute-start | bytes 331784 | tf_op jit(solution)/shard_map/ppermute | solution.py:364
  67.1 5.8 %collective-permute-start.5 = (bf16[2,216,128]{2,1,0:T(8,128)(2,1)S(1)}, bf16[2,216,128]{2,1,0:T(8,128)(2,1)S(1)}, u32[]{:S(2)}, u32[]{:S(2)}) collective-permute-start(bf16[2,216,128]{2,1,0:T(8,128)(2,1)S(1)} %get-tuple-element.70), channel_id=1, source_target_pairs={{0,5},{1,6},{2,7},{3,0},{4,1},{5,2},{6,3},{7,4},{8,13},{9,14},{10,... | collective-permute-start | bytes 331784 | tf_op jit(solution)/shard_map/ppermute | solution.py:364
  72.9 2.1 collective-permute-done.3.refs_3_
  75.0 1.9 collective-permute-start.6
  76.9 2.8 %collective-permute-start.7 = (bf16[2,216,128]{2,1,0:T(8,128)(2,1)S(1)}, bf16[2,216,128]{2,1,0:T(8,128)(2,1)S(1)}, u32[]{:S(2)}, u32[]{:S(2)}) collective-permute-start(bf16[2,216,128]{2,1,0:T(8,128)(2,1)S(1)} %get-tuple-element.72), channel_id=1, source_target_pairs={{0,7},{1,0},{2,1},{3,2},{4,3},{5,4},{6,5},{7,6},{8,15},{9,8},{10,9... | collective-permute-start | bytes 331784 | tf_op jit(solution)/shard_map/ppermute | solution.py:364
  79.7 5.3 %collective-permute-done.5.refs_5_ = bf16[2,216,128]{2,1,0:T(8,128)(2,1)S(1)} collective-permute-done((bf16[2,216,128]{2,1,0:T(8,128)(2,1)S(1)}, bf16[2,216,128]{2,1,0:T(8,128)(2,1)S(1)}, u32[]{:S(2)}, u32[]{:S(2)}) %collective-permute-start.5) | collective-permute-done | bytes 110624 | tf_op jit(solution)/shard_map/ppermute | solution.py:364
  85.1 3.0 %collective-permute-done.7.refs_7_ = bf16[2,216,128]{2,1,0:T(8,128)(2,1)S(1)} collective-permute-done((bf16[2,216,128]{2,1,0:T(8,128)(2,1)S(1)}, bf16[2,216,128]{2,1,0:T(8,128)(2,1)S(1)}, u32[]{:S(2)}, u32[]{:S(2)}) %collective-permute-start.7) | collective-permute-done | bytes 110624 | tf_op jit(solution)/shard_map/ppermute | solution.py:364
  89.4 1.9 reshape.59.own_ref
  91.2 3.3 %collective-permute-start.9 = (bf16[288,1152]{1,0:T(8,128)(2,1)S(1)}, bf16[288,1152]{1,0:T(8,128)(2,1)S(1)}, u32[]{:S(2)}, u32[]{:S(2)}) collective-permute-start(bf16[288,1152]{1,0:T(8,128)(2,1)S(1)} %reshape.59.own_ref), channel_id=1, source_target_pairs={{0,16},{16,0},{1,17},{17,1},{2,18},{18,2},{3,19},{19,3},{4,20},{20... | collective-permute-start | bytes 1990664 | tf_op jit(solution)/shard_map/ppermute | solution.py:369
  94.6 1.7 add_convert_fusion
  97.7 3.1 %collective-permute-start.11 = (bf16[576,640]{1,0:T(8,128)(2,1)}, bf16[576,640]{1,0:T(8,128)(2,1)S(1)}, u32[]{:S(2)}, u32[]{:S(2)}) collective-permute-start(bf16[576,640]{1,0:T(8,128)(2,1)} %dynamic-slice_bitcast_fusion), channel_id=1, source_target_pairs={{0,8},{8,0},{1,9},{9,1},{2,10},{10,2},{3,11},{11,3},{4,12},{12,4},... | collective-permute-start | bytes 2211848 | tf_op jit(solution)/shard_map/ppermute | solution.py:380
  100.9 2.0 project.1
  102.8 5.0 %all-to-all-start.2 = ((bf16[16,80,128]{2,1,0:T(8,128)(2,1)}), bf16[16,80,128]{2,1,0:T(8,128)(2,1)S(1)}, u32[]{:S(2)}, u32[]{:S(2)}) async-start(bf16[16,80,128]{2,1,0:T(8,128)(2,1)} %project.1), calls=%async_computation.2 | async-start | bytes 655360 | tf_op jit(solution)/shard_map/all_to_all | solution.py:321
  107.8 10.8 %probs.1.probs_ref = bf16[2048,2048]{1,0:T(8,128)(2,1)} custom-call(bf16[16,3,72,128]{3,2,1,0:T(8,128)(2,1)S(1)} %bitcast.35), custom_call_target="tpu_custom_call" | custom-call | flops 2147483648 | bytes 8388608 | tf_op jit(solution)/shard_map/probs/pallas_call | solution.py:123
  118.6 2.3 %collective-permute-done.11 = bf16[576,640]{1,0:T(8,128)(2,1)S(1)} collective-permute-done((bf16[576,640]{1,0:T(8,128)(2,1)}, bf16[576,640]{1,0:T(8,128)(2,1)S(1)}, u32[]{:S(2)}, u32[]{:S(2)}) %collective-permute-start.11) | collective-permute-done | bytes 737312 | tf_op jit(solution)/shard_map/ppermute | solution.py:380
  121.0 1.1 fusion
  122.0 5.0 %all-to-all-start.3 = ((bf16[8,72,640]{2,1,0:T(8,128)(2,1)}), bf16[8,72,640]{2,1,0:T(8,128)(2,1)S(1)}, u32[]{:S(2)}, u32[]{:S(2)}) async-start(bf16[8,72,640]{2,1,0:T(8,128)(2,1)} %bitcast.16), calls=%async_computation.3 | async-start | bytes 1474560 | tf_op jit(solution)/shard_map/all_to_all | solution.py:321
  127.0 16.0 %grads.1 = bf16[16,3,72,128]{3,2,1,0:T(8,128)(2,1)} custom-call(bf16[16,3,72,128]{3,2,1,0:T(8,128)(2,1)S(1)} %bitcast.36, bf16[16,80,128]{2,1,0:T(8,128)(2,1)S(1)} %all-to-all-done.2.grad_ref, bf16[2048,2048]{1,0:T(8,128)(2,1)} %probs.1.probs_ref), custom_call_target="tpu_custom_call" | custom-call | flops 8589934592 | bytes 8388608 | tf_op jit(solution)/shard_map/grads/pallas_call | solution.py:142
  143.0 1.4 all-to-all-done.3.clip_ref
  144.4 8.6 %all-to-all-start.4 = ((bf16[16,3,72,128]{3,2,1,0:T(8,128)(2,1)}), bf16[16,3,72,128]{3,2,1,0:T(8,128)(2,1)S(1)}, u32[]{:S(2)}, u32[]{:S(2)}) async-start(bf16[16,3,72,128]{3,2,1,0:T(8,128)(2,1)} %grads.1), calls=%async_computation.4 | async-start | bytes 1769472 | tf_op jit(solution)/shard_map/all_to_all | solution.py:321
  153.7 3.1 %collective-permute-start.12 = (f32[4,24,128]{2,1,0:T(8,128)S(1)}, f32[4,24,128]{2,1,0:T(8,128)S(1)}, u32[]{:S(2)}, u32[]{:S(2)}) collective-permute-start(f32[4,24,128]{2,1,0:T(8,128)S(1)} %get-tuple-element.88), channel_id=1, source_target_pairs={{0,32},{32,64},{64,96},{96,128},{128,160},{160,192},{192,224},{224... | collective-permute-start | bytes 147464 | tf_op jit(solution)/shard_map/ppermute | solution.py:394
  156.8 4.3 %collective-permute-start.13 = (f32[4,24,128]{2,1,0:T(8,128)S(1)}, f32[4,24,128]{2,1,0:T(8,128)S(1)}, u32[]{:S(2)}, u32[]{:S(2)}) collective-permute-start(f32[4,24,128]{2,1,0:T(8,128)S(1)} %get-tuple-element.89), channel_id=1, source_target_pairs={{0,64},{32,96},{64,128},{96,160},{128,192},{160,224},{192,0},{224,... | collective-permute-start | bytes 147464 | tf_op jit(solution)/shard_map/ppermute | solution.py:394
  161.1 2.2 collective-permute-start.14
  163.3 7.0 %collective-permute-start.15 = (f32[4,24,128]{2,1,0:T(8,128)S(1)}, f32[4,24,128]{2,1,0:T(8,128)S(1)}, u32[]{:S(2)}, u32[]{:S(2)}) collective-permute-start(f32[4,24,128]{2,1,0:T(8,128)S(1)} %get-tuple-element.91), channel_id=1, source_target_pairs={{0,128},{32,160},{64,192},{96,224},{128,0},{160,32},{192,64},{224,... | collective-permute-start | bytes 147464 | tf_op jit(solution)/shard_map/ppermute | solution.py:394
  170.4 2.2 collective-permute-start.16
  172.6 3.1 %collective-permute-start.17 = (f32[4,24,128]{2,1,0:T(8,128)S(1)}, f32[4,24,128]{2,1,0:T(8,128)S(1)}, u32[]{:S(2)}, u32[]{:S(2)}) collective-permute-start(f32[4,24,128]{2,1,0:T(8,128)S(1)} %get-tuple-element.93), channel_id=1, source_target_pairs={{0,192},{32,224},{64,0},{96,32},{128,64},{160,96},{192,128},{224,1... | collective-permute-start | bytes 147464 | tf_op jit(solution)/shard_map/ppermute | solution.py:394
  175.7 3.1 %collective-permute-start.18 = (f32[4,24,128]{2,1,0:T(8,128)S(1)}, f32[4,24,128]{2,1,0:T(8,128)S(1)}, u32[]{:S(2)}, u32[]{:S(2)}) collective-permute-start(f32[4,24,128]{2,1,0:T(8,128)S(1)} %get-tuple-element.94), channel_id=1, source_target_pairs={{0,224},{32,0},{64,32},{96,64},{128,96},{160,128},{192,160},{224,1... | collective-permute-start | bytes 147464 | tf_op jit(solution)/shard_map/ppermute | solution.py:394
  178.8 1.1 collective-permute-done.17.refs_6_
  179.9 1.3 collective-permute-done.18.refs_7_
  181.8 10.5 %collective-permute-start.19 = (f32[24,128]{1,0:T(8,128)S(1)}, f32[24,128]{1,0:T(8,128)S(1)}, u32[]{:S(2)}, u32[]{:S(2)}) collective-permute-start(f32[24,128]{1,0:T(8,128)S(1)} %get-tuple-element.95), channel_id=1, source_target_pairs={{0,0},{16,512},{32,16},{48,528},{64,32},{80,544},{96,48},{112,560}... | collective-permute-start | bytes 36872 | tf_op jit(solution)/shard_map/ppermute | solution.py:406
  192.2 2.2 %collective-permute-start.20 = (f32[24,128]{1,0:T(8,128)S(1)}, f32[24,128]{1,0:T(8,128)S(1)}, u32[]{:S(2)}, u32[]{:S(2)}) collective-permute-start(f32[24,128]{1,0:T(8,128)S(1)} %get-tuple-element.96), channel_id=1, source_target_pairs={{0,128},{16,640},{32,144},{48,656},{64,160},{80,672},{96,176},{112... | collective-permute-start | bytes 36872 | tf_op jit(solution)/shard_map/ppermute | solution.py:406
  194.5 9.9 %collective-permute-start.21 = (f32[24,128]{1,0:T(8,128)S(1)}, f32[24,128]{1,0:T(8,128)S(1)}, u32[]{:S(2)}, u32[]{:S(2)}) collective-permute-start(f32[24,128]{1,0:T(8,128)S(1)} %get-tuple-element.97), channel_id=1, source_target_pairs={{0,256},{16,768},{32,272},{48,784},{64,288},{80,800},{96,304},{112... | collective-permute-start | bytes 36872 | tf_op jit(solution)/shard_map/ppermute | solution.py:406
  204.4 2.2 %collective-permute-start.22 = (f32[24,128]{1,0:T(8,128)S(1)}, f32[24,128]{1,0:T(8,128)S(1)}, u32[]{:S(2)}, u32[]{:S(2)}) collective-permute-start(f32[24,128]{1,0:T(8,128)S(1)} %get-tuple-element.98), channel_id=1, source_target_pairs={{0,384},{16,896},{32,400},{48,912},{64,416},{80,928},{96,432},{112... | collective-permute-start | bytes 36872 | tf_op jit(solution)/shard_map/ppermute | solution.py:406
  206.7 10.6 %collective-permute-done.22 = f32[24,128]{1,0:T(8,128)S(1)} collective-permute-done((f32[24,128]{1,0:T(8,128)S(1)}, f32[24,128]{1,0:T(8,128)S(1)}, u32[]{:S(2)}, u32[]{:S(2)}) %collective-permute-start.22) | collective-permute-done | bytes 12320 | tf_op jit(solution)/shard_map/ppermute | solution.py:406
  217.9 1.5 copy.22
  (62 shorter events, 8.4 us)
Async XLA Ops:
  4.6 21.7 %copy-start = (bf16[128,1152]{1,0:T(8,128)(2,1)S(1)}, bf16[128,1152]{1,0:T(8,128)(2,1)}, u32[]{:S(2)}) copy-start(bf16[128,1152]{1,0:T(8,128)(2,1)} %refs_2_) | copy-start | bytes 884740
  4.7 21.7 %copy-start.1 = (bf16[128,1152]{1,0:T(8,128)(2,1)S(1)}, bf16[128,1152]{1,0:T(8,128)(2,1)}, u32[]{:S(2)}) copy-start(bf16[128,1152]{1,0:T(8,128)(2,1)} %refs_1_) | copy-start | bytes 884740
  4.7 19.1 %collective-permute-start = (bf16[8,216,128]{2,1,0:T(8,128)(2,1)S(1)}, bf16[8,216,128]{2,1,0:T(8,128)(2,1)S(1)}, u32[]{:S(2)}, u32[]{:S(2)}) collective-permute-start(bf16[8,216,128]{2,1,0:T(8,128)(2,1)S(1)} %dynamic-slice_bitcast_fusion.1), channel_id=1, source_target_pairs={{0,8},{8,0},{1,9},{9,1},{2,10},{10,2},{3,11},{11,3},{4,12},{12,4},... | collective-permute-start | bytes 1327112 | tf_op jit(solution)/shard_map/ppermute | solution.py:352
  9.8 13.7 %all-to-all-start = ((bf16[16,8,128]{2,1,0:T(8,128)(2,1)}), bf16[16,8,128]{2,1,0:T(8,128)(2,1)S(1)}, u32[]{:S(2)}, u32[]{:S(2)}) async-start(bf16[16,8,128]{2,1,0:T(8,128)(2,1)} %bitcast.1), calls=%async_computation | async-start | bytes 65536 | tf_op jit(solution)/shard_map/all_to_all | solution.py:321
  24.4 0.6 copy-start.4
  25.1 0.7 copy-start.6
  25.7 0.6 copy-start.8
  29.3 21.7 %copy-start.9 = (bf16[2,216,128]{2,1,0:T(8,128)(2,1)S(1)}, bf16[2,216,128]{2,1,0:T(8,128)(2,1)}, u32[]{:S(2)}) copy-start(bf16[2,216,128]{2,1,0:T(8,128)(2,1)} %copy-done.8) | copy-start | bytes 331780
  29.3 26.3 %copy-start.7 = (bf16[2,216,128]{2,1,0:T(8,128)(2,1)S(1)}, bf16[2,216,128]{2,1,0:T(8,128)(2,1)}, u32[]{:S(2)}) copy-start(bf16[2,216,128]{2,1,0:T(8,128)(2,1)} %copy-done.6) | copy-start | bytes 331780
  29.3 29.4 %copy-start.5 = (bf16[2,216,128]{2,1,0:T(8,128)(2,1)S(1)}, bf16[2,216,128]{2,1,0:T(8,128)(2,1)}, u32[]{:S(2)}) copy-start(bf16[2,216,128]{2,1,0:T(8,128)(2,1)} %copy-done.4) | copy-start | bytes 331780
  29.3 65.2 %collective-permute-start.10 = (bf16[1152,640]{1,0:T(8,128)(2,1)}, bf16[1152,640]{1,0:T(8,128)(2,1)}, u32[]{:S(2)}, u32[]{:S(2)}) collective-permute-start(bf16[1152,640]{1,0:T(8,128)(2,1)} %get-tuple-element.80), channel_id=1, source_target_pairs={{0,16},{16,0},{1,17},{17,1},{2,18},{18,2},{3,19},{19,3},{4,20},{20... | collective-permute-start | bytes 4423688 | tf_op jit(solution)/shard_map/ppermute | solution.py:377
  34.7 54.6 %all-to-all-start.1 = ((bf16[32,81,128]{2,1,0:T(8,128)(2,1)}), bf16[32,81,128]{2,1,0:T(8,128)(2,1)}, u32[]{:S(2)}, u32[]{:S(2)}) async-start(bf16[32,81,128]{2,1,0:T(8,128)(2,1)} %broadcast_in_dim.19), calls=%async_computation.1 | async-start | bytes 1441792 | tf_op jit(solution)/shard_map/all_to_all | solution.py:321
  51.0 11.7 %collective-permute-start.1 = (bf16[2,216,128]{2,1,0:T(8,128)(2,1)S(1)}, bf16[2,216,128]{2,1,0:T(8,128)(2,1)S(1)}, u32[]{:S(2)}, u32[]{:S(2)}) collective-permute-start(bf16[2,216,128]{2,1,0:T(8,128)(2,1)S(1)} %copy-done.9), channel_id=1, source_target_pairs={{0,1},{1,2},{2,3},{3,4},{4,5},{5,6},{6,7},{7,0},{8,9},{9,10},{10,1... | collective-permute-start | bytes 331784 | tf_op jit(solution)/shard_map/ppermute | solution.py:364
  53.4 35.2 %collective-permute-start.8 = (bf16[128,1152]{1,0:T(8,128)(2,1)S(1)}, bf16[128,1152]{1,0:T(8,128)(2,1)S(1)}, u32[]{:S(2)}, u32[]{:S(2)}) collective-permute-start(bf16[128,1152]{1,0:T(8,128)(2,1)S(1)} %copy-done.1), channel_id=1, source_target_pairs={{0,8},{8,0},{1,9},{9,1},{2,10},{10,2},{3,11},{11,3},{4,12},{12,4},... | collective-permute-start | bytes 884744 | tf_op jit(solution)/shard_map/ppermute | solution.py:360
  55.7 11.4 %collective-permute-start.2 = (bf16[2,216,128]{2,1,0:T(8,128)(2,1)S(1)}, bf16[2,216,128]{2,1,0:T(8,128)(2,1)S(1)}, u32[]{:S(2)}, u32[]{:S(2)}) collective-permute-start(bf16[2,216,128]{2,1,0:T(8,128)(2,1)S(1)} %copy-done.7), channel_id=1, source_target_pairs={{0,2},{1,3},{2,4},{3,5},{4,6},{5,7},{6,0},{7,1},{8,10},{9,11},{10,... | collective-permute-start | bytes 331784 | tf_op jit(solution)/shard_map/ppermute | solution.py:364
  58.8 16.2 %collective-permute-start.3 = (bf16[2,216,128]{2,1,0:T(8,128)(2,1)S(1)}, bf16[2,216,128]{2,1,0:T(8,128)(2,1)S(1)}, u32[]{:S(2)}, u32[]{:S(2)}) collective-permute-start(bf16[2,216,128]{2,1,0:T(8,128)(2,1)S(1)} %copy-done.5), channel_id=1, source_target_pairs={{0,3},{1,4},{2,5},{3,6},{4,7},{5,0},{6,1},{7,2},{8,11},{9,12},{10,... | collective-permute-start | bytes 331784 | tf_op jit(solution)/shard_map/ppermute | solution.py:364
  62.8 14.2 %collective-permute-start.4 = (bf16[2,216,128]{2,1,0:T(8,128)(2,1)S(1)}, bf16[2,216,128]{2,1,0:T(8,128)(2,1)S(1)}, u32[]{:S(2)}, u32[]{:S(2)}) collective-permute-start(bf16[2,216,128]{2,1,0:T(8,128)(2,1)S(1)} %get-tuple-element.69), channel_id=1, source_target_pairs={{0,4},{1,5},{2,6},{3,7},{4,0},{5,1},{6,2},{7,3},{8,12},{9,13},{10,... | collective-permute-start | bytes 331784 | tf_op jit(solution)/shard_map/ppermute | solution.py:364
  67.1 17.9 %collective-permute-start.5 = (bf16[2,216,128]{2,1,0:T(8,128)(2,1)S(1)}, bf16[2,216,128]{2,1,0:T(8,128)(2,1)S(1)}, u32[]{:S(2)}, u32[]{:S(2)}) collective-permute-start(bf16[2,216,128]{2,1,0:T(8,128)(2,1)S(1)} %get-tuple-element.70), channel_id=1, source_target_pairs={{0,5},{1,6},{2,7},{3,0},{4,1},{5,2},{6,3},{7,4},{8,13},{9,14},{10,... | collective-permute-start | bytes 331784 | tf_op jit(solution)/shard_map/ppermute | solution.py:364
  75.0 10.0 %collective-permute-start.6 = (bf16[2,216,128]{2,1,0:T(8,128)(2,1)S(1)}, bf16[2,216,128]{2,1,0:T(8,128)(2,1)S(1)}, u32[]{:S(2)}, u32[]{:S(2)}) collective-permute-start(bf16[2,216,128]{2,1,0:T(8,128)(2,1)S(1)} %get-tuple-element.71), channel_id=1, source_target_pairs={{0,6},{1,7},{2,0},{3,1},{4,2},{5,3},{6,4},{7,5},{8,14},{9,15},{10,... | collective-permute-start | bytes 331784 | tf_op jit(solution)/shard_map/ppermute | solution.py:364
  76.9 11.1 %collective-permute-start.7 = (bf16[2,216,128]{2,1,0:T(8,128)(2,1)S(1)}, bf16[2,216,128]{2,1,0:T(8,128)(2,1)S(1)}, u32[]{:S(2)}, u32[]{:S(2)}) collective-permute-start(bf16[2,216,128]{2,1,0:T(8,128)(2,1)S(1)} %get-tuple-element.72), channel_id=1, source_target_pairs={{0,7},{1,0},{2,1},{3,2},{4,3},{5,4},{6,5},{7,6},{8,15},{9,8},{10,9... | collective-permute-start | bytes 331784 | tf_op jit(solution)/shard_map/ppermute | solution.py:364
  88.6 0.7 copy-start.2
  91.2 9.6 %collective-permute-start.9 = (bf16[288,1152]{1,0:T(8,128)(2,1)S(1)}, bf16[288,1152]{1,0:T(8,128)(2,1)S(1)}, u32[]{:S(2)}, u32[]{:S(2)}) collective-permute-start(bf16[288,1152]{1,0:T(8,128)(2,1)S(1)} %reshape.59.own_ref), channel_id=1, source_target_pairs={{0,16},{16,0},{1,17},{17,1},{2,18},{18,2},{3,19},{19,3},{4,20},{20... | collective-permute-start | bytes 1990664 | tf_op jit(solution)/shard_map/ppermute | solution.py:369
  96.3 1.4 copy-start.10
  96.3 4.5 %copy-start.3 = (bf16[128,1152]{1,0:T(8,128)(2,1)S(1)}, bf16[128,1152]{1,0:T(8,128)(2,1)}, u32[]{:S(2)}) copy-start(bf16[128,1152]{1,0:T(8,128)(2,1)} %copy-done.2) | copy-start | bytes 884740
  97.7 23.3 %collective-permute-start.11 = (bf16[576,640]{1,0:T(8,128)(2,1)}, bf16[576,640]{1,0:T(8,128)(2,1)S(1)}, u32[]{:S(2)}, u32[]{:S(2)}) collective-permute-start(bf16[576,640]{1,0:T(8,128)(2,1)} %dynamic-slice_bitcast_fusion), channel_id=1, source_target_pairs={{0,8},{8,0},{1,9},{9,1},{2,10},{10,2},{3,11},{11,3},{4,12},{12,4},... | collective-permute-start | bytes 2211848 | tf_op jit(solution)/shard_map/ppermute | solution.py:380
  102.8 19.2 %all-to-all-start.2 = ((bf16[16,80,128]{2,1,0:T(8,128)(2,1)}), bf16[16,80,128]{2,1,0:T(8,128)(2,1)S(1)}, u32[]{:S(2)}, u32[]{:S(2)}) async-start(bf16[16,80,128]{2,1,0:T(8,128)(2,1)} %project.1), calls=%async_computation.2 | async-start | bytes 655360 | tf_op jit(solution)/shard_map/all_to_all | solution.py:321
  107.8 13.2 %copy-start.11 = (bf16[1152,640]{1,0:T(8,128)(2,1)S(1)}, bf16[1152,640]{1,0:T(8,128)(2,1)}, u32[]{:S(2)}) copy-start(bf16[1152,640]{1,0:T(8,128)(2,1)} %copy-done.10) | copy-start | bytes 4423684
  122.0 22.4 %all-to-all-start.3 = ((bf16[8,72,640]{2,1,0:T(8,128)(2,1)}), bf16[8,72,640]{2,1,0:T(8,128)(2,1)S(1)}, u32[]{:S(2)}, u32[]{:S(2)}) async-start(bf16[8,72,640]{2,1,0:T(8,128)(2,1)} %bitcast.16), calls=%async_computation.3 | async-start | bytes 1474560 | tf_op jit(solution)/shard_map/all_to_all | solution.py:321
  144.4 73.4 %all-to-all-start.4 = ((bf16[16,3,72,128]{3,2,1,0:T(8,128)(2,1)}), bf16[16,3,72,128]{3,2,1,0:T(8,128)(2,1)S(1)}, u32[]{:S(2)}, u32[]{:S(2)}) async-start(bf16[16,3,72,128]{3,2,1,0:T(8,128)(2,1)} %grads.1), calls=%async_computation.4 | async-start | bytes 1769472 | tf_op jit(solution)/shard_map/all_to_all | solution.py:321
  153.7 18.8 %collective-permute-start.12 = (f32[4,24,128]{2,1,0:T(8,128)S(1)}, f32[4,24,128]{2,1,0:T(8,128)S(1)}, u32[]{:S(2)}, u32[]{:S(2)}) collective-permute-start(f32[4,24,128]{2,1,0:T(8,128)S(1)} %get-tuple-element.88), channel_id=1, source_target_pairs={{0,32},{32,64},{64,96},{96,128},{128,160},{160,192},{192,224},{224... | collective-permute-start | bytes 147464 | tf_op jit(solution)/shard_map/ppermute | solution.py:394
  156.8 18.8 %collective-permute-start.13 = (f32[4,24,128]{2,1,0:T(8,128)S(1)}, f32[4,24,128]{2,1,0:T(8,128)S(1)}, u32[]{:S(2)}, u32[]{:S(2)}) collective-permute-start(f32[4,24,128]{2,1,0:T(8,128)S(1)} %get-tuple-element.89), channel_id=1, source_target_pairs={{0,64},{32,96},{64,128},{96,160},{128,192},{160,224},{192,0},{224,... | collective-permute-start | bytes 147464 | tf_op jit(solution)/shard_map/ppermute | solution.py:394
  161.1 17.6 %collective-permute-start.14 = (f32[4,24,128]{2,1,0:T(8,128)S(1)}, f32[4,24,128]{2,1,0:T(8,128)S(1)}, u32[]{:S(2)}, u32[]{:S(2)}) collective-permute-start(f32[4,24,128]{2,1,0:T(8,128)S(1)} %get-tuple-element.90), channel_id=1, source_target_pairs={{0,96},{32,128},{64,160},{96,192},{128,224},{160,0},{192,32},{224,... | collective-permute-start | bytes 147464 | tf_op jit(solution)/shard_map/ppermute | solution.py:394
  163.3 15.4 %collective-permute-start.15 = (f32[4,24,128]{2,1,0:T(8,128)S(1)}, f32[4,24,128]{2,1,0:T(8,128)S(1)}, u32[]{:S(2)}, u32[]{:S(2)}) collective-permute-start(f32[4,24,128]{2,1,0:T(8,128)S(1)} %get-tuple-element.91), channel_id=1, source_target_pairs={{0,128},{32,160},{64,192},{96,224},{128,0},{160,32},{192,64},{224,... | collective-permute-start | bytes 147464 | tf_op jit(solution)/shard_map/ppermute | solution.py:394
  170.4 8.5 %collective-permute-start.16 = (f32[4,24,128]{2,1,0:T(8,128)S(1)}, f32[4,24,128]{2,1,0:T(8,128)S(1)}, u32[]{:S(2)}, u32[]{:S(2)}) collective-permute-start(f32[4,24,128]{2,1,0:T(8,128)S(1)} %get-tuple-element.92), channel_id=1, source_target_pairs={{0,160},{32,192},{64,224},{96,0},{128,32},{160,64},{192,96},{224,1... | collective-permute-start | bytes 147464 | tf_op jit(solution)/shard_map/ppermute | solution.py:394
  172.6 7.3 %collective-permute-start.17 = (f32[4,24,128]{2,1,0:T(8,128)S(1)}, f32[4,24,128]{2,1,0:T(8,128)S(1)}, u32[]{:S(2)}, u32[]{:S(2)}) collective-permute-start(f32[4,24,128]{2,1,0:T(8,128)S(1)} %get-tuple-element.93), channel_id=1, source_target_pairs={{0,192},{32,224},{64,0},{96,32},{128,64},{160,96},{192,128},{224,1... | collective-permute-start | bytes 147464 | tf_op jit(solution)/shard_map/ppermute | solution.py:394
  175.7 5.5 %collective-permute-start.18 = (f32[4,24,128]{2,1,0:T(8,128)S(1)}, f32[4,24,128]{2,1,0:T(8,128)S(1)}, u32[]{:S(2)}, u32[]{:S(2)}) collective-permute-start(f32[4,24,128]{2,1,0:T(8,128)S(1)} %get-tuple-element.94), channel_id=1, source_target_pairs={{0,224},{32,0},{64,32},{96,64},{128,96},{160,128},{192,160},{224,1... | collective-permute-start | bytes 147464 | tf_op jit(solution)/shard_map/ppermute | solution.py:394
  181.8 24.9 %collective-permute-start.19 = (f32[24,128]{1,0:T(8,128)S(1)}, f32[24,128]{1,0:T(8,128)S(1)}, u32[]{:S(2)}, u32[]{:S(2)}) collective-permute-start(f32[24,128]{1,0:T(8,128)S(1)} %get-tuple-element.95), channel_id=1, source_target_pairs={{0,0},{16,512},{32,16},{48,528},{64,32},{80,544},{96,48},{112,560}... | collective-permute-start | bytes 36872 | tf_op jit(solution)/shard_map/ppermute | solution.py:406
  192.2 14.4 %collective-permute-start.20 = (f32[24,128]{1,0:T(8,128)S(1)}, f32[24,128]{1,0:T(8,128)S(1)}, u32[]{:S(2)}, u32[]{:S(2)}) collective-permute-start(f32[24,128]{1,0:T(8,128)S(1)} %get-tuple-element.96), channel_id=1, source_target_pairs={{0,128},{16,640},{32,144},{48,656},{64,160},{80,672},{96,176},{112... | collective-permute-start | bytes 36872 | tf_op jit(solution)/shard_map/ppermute | solution.py:406
  194.5 12.2 %collective-permute-start.21 = (f32[24,128]{1,0:T(8,128)S(1)}, f32[24,128]{1,0:T(8,128)S(1)}, u32[]{:S(2)}, u32[]{:S(2)}) collective-permute-start(f32[24,128]{1,0:T(8,128)S(1)} %get-tuple-element.97), channel_id=1, source_target_pairs={{0,256},{16,768},{32,272},{48,784},{64,288},{80,800},{96,304},{112... | collective-permute-start | bytes 36872 | tf_op jit(solution)/shard_map/ppermute | solution.py:406
  204.4 12.8 %collective-permute-start.22 = (f32[24,128]{1,0:T(8,128)S(1)}, f32[24,128]{1,0:T(8,128)S(1)}, u32[]{:S(2)}, u32[]{:S(2)}) collective-permute-start(f32[24,128]{1,0:T(8,128)S(1)} %get-tuple-element.98), channel_id=1, source_target_pairs={{0,384},{16,896},{32,400},{48,912},{64,416},{80,928},{96,432},{112... | collective-permute-start | bytes 36872 | tf_op jit(solution)/shard_map/ppermute | solution.py:406

commit v3 on v1

--- a/solution.py
+++ b/solution.py
@@ -1,3 +1,5 @@
+import math
+
 import jax
 import jax.numpy as jnp
 from jax import lax
@@ -246,9 +248,37 @@
     )(core, own, other, dout, near)
 
 
+def arrange_kernel(clip_ref, out_ref):
+    line, across = out_ref.shape[0], out_ref.shape[1]
+    cols = clip_ref.shape[1]
+    total = clip_ref[0].astype(jnp.float32)
+    for s in range(1, clip_ref.shape[0]):
+        total = total + clip_ref[s].astype(jnp.float32)
+    turned = total.T
+    out_ref[...] = jnp.zeros_like(out_ref)
+    for z in range(across):
+        for x in range(line):
+            start = (z * line + x) * ROWS_DEV
+            out_ref[x, z, :ROWS_DEV, :cols] = turned[start : start + ROWS_DEV]
+
+
+def arrange_call(clip, line, across):
+    vmem = pl.BlockSpec(memory_space=pltpu.VMEM)
+    return pl.pallas_call(
+        arrange_kernel,
+        out_shape=jax.ShapeDtypeStruct((line, across, 24, LANES), jnp.float32),
+        in_specs=[vmem],
+        out_specs=vmem,
+        compiler_params=pltpu.CompilerParams(vmem_limit_bytes=16 * 2**20),
+        cost_estimate=pl.CostEstimate(flops=0, transcendentals=0, bytes_accessed=0),
+        name="arrange",
+    )(clip)
+
+
 SEQ = ("zl", "y")
 ROWS = ("zh", "x")
 DP = ("zh", "x", "c")
+ROWS_DEV = 18
 SHARE = 9
 LANES = 128
 SWAP = [(0, 1), (1, 0)]
@@ -256,14 +286,19 @@
 
 def exchange(array, axes):
     return lax.all_to_all(array, axes, 0, 0, tiled=True)
+
+
+def at(array, index):
+    return lax.dynamic_index_in_dim(array, index, 0, keepdims=False)
 
 
 def per_device(qkv, attn_out, dout, w_master, mom1, mom2, grad_prev):
     tokens, _, width = qkv.shape
     seq_count = lax.axis_size(SEQ)
     row_count = lax.axis_size(ROWS)
+    ring = lax.axis_size("y")
     rows, cols = w_master.shape
-    core = lax.axis_index("c")
+    core, side = lax.axis_index("c"), lax.axis_index("zl")
     core_id = core[None].astype(jnp.int32)
 
     moment_one = BETA_ONE * mom1 + (1.0 - BETA_ONE) * grad_prev
@@ -279,7 +314,6 @@
     flat = jnp.broadcast_to(flat, (2, seq_count // 2, 8, LANES)).reshape(seq_count, 8, LANES)
     packed = jnp.concatenate([by_head, flat], axis=1)
     packed, dout, attn_out = lax.optimization_barrier((packed, dout, attn_out))
-    near = lax.ppermute(dout, "zl", SWAP)
     arrived = exchange(packed, SEQ)
     heads_qkv = arrived[:, : 3 * HD].reshape(seq_count, 3, HD, tokens)
     columns = arrived[:, 3 * HD :].reshape(seq_count, 8 * LANES)[:, :size].reshape(seq_count, SHARE, cols)
@@ -288,23 +322,39 @@
     kept, sent = term_call(core_id, dout, attn_out, factor)
     sent = lax.ppermute(sent, "c", SWAP)
     pair = (kept.astype(jnp.float32) + sent.astype(jnp.float32)).astype(jnp.bfloat16)
-
-    row_block = jnp.transpose(columns, (1, 0, 2)).reshape(SHARE * width // LANES, LANES)
-    row_block, pair, near = lax.optimization_barrier((row_block, pair, near))
+    pair = pair.reshape(2, width // 2, pair.shape[1])
+    sent = lax.ppermute(at(pair, 1 - side), "zl", SWAP)
+    quad = (at(pair, side).astype(jnp.float32) + sent.astype(jnp.float32)).astype(jnp.bfloat16)
+
+    lane = math.gcd(SHARE * width, LANES)
+    row_block = jnp.transpose(columns, (1, 0, 2)).reshape(SHARE * width // lane, lane)
+    near = lax.ppermute(dout, "zl", SWAP)
+    row_block, quad, near = lax.optimization_barrier((row_block, quad, near))
     own = exchange(jnp.broadcast_to(row_block[None], (row_count,) + row_block.shape), ROWS)
     probs = probs_call(heads_qkv)
-    own, probs = lax.optimization_barrier((own, probs))
+    own, probs, near = lax.optimization_barrier((own, probs, near))
     own = own.reshape(row_count * SHARE, width)
     other = lax.ppermute(own, "c", SWAP)
     grad_rows = project_call(core_id, own, other, dout, near, seq_count)
     heads_grad = exchange(grad_rows, SEQ)
 
-    clip = lax.psum_scatter(pair, SEQ, scatter_dimension=0, tiled=True)
-    clip, heads_grad = lax.optimization_barrier((clip, heads_grad))
+    quad, heads_grad, probs = lax.optimization_barrier((quad, heads_grad, probs))
+    clip = exchange(quad.reshape(ring, cols, quad.shape[1]), "y")
+    local = grads_call(heads_qkv, heads_grad, probs)
+    local, clip = lax.optimization_barrier((local, clip))
+
     line, across = lax.axis_size("x"), lax.axis_size("zh")
-    pieces = jnp.transpose(clip[:, : width // 2].T.reshape(across, line, rows * cols), (1, 0, 2))
-    pieces = jnp.sum(exchange(pieces, "x").astype(jnp.float32), axis=0)
-    grad_new = jnp.zeros((rows * cols,), jnp.float32)
+    pieces = arrange_call(clip, line, across)
+    reach = line // 2
+    while reach:
+        bit = (lax.axis_index("x") // reach) % 2
+        halves = pieces.reshape((2, reach) + pieces.shape[1:])
+        sent = at(halves, 1 - bit).astype(jnp.bfloat16)
+        sent = lax.ppermute(sent, "x", [(i, i ^ reach) for i in range(line)])
+        pieces = at(halves, bit) + sent.astype(jnp.float32)
+        reach //= 2
+    pieces = pieces[0]
+    grad_new = jnp.zeros((24, LANES), jnp.float32)
     for turn in range(across):
         moves = [
             ((z * line + x) * 2 + c, (c * across + (z + turn) % across) * line + x)
@@ -312,11 +362,9 @@
             for x in range(line)
             for c in range(2)
         ]
-        piece = lax.dynamic_slice_in_dim(pieces, (lax.axis_index("zh") + turn) % across, 1, 0)[0]
-        grad_new = grad_new + lax.ppermute(piece, DP, moves)
-    grad_new = grad_new.reshape(rows, cols)
-
-    local = grads_call(heads_qkv, heads_grad, probs)
+        grad_new = grad_new + lax.ppermute(at(pieces, (lax.axis_index("zh") + turn) % across), DP, moves)
+    grad_new = grad_new[:rows, :cols]
+
     back = exchange(local, SEQ)
     dqkv = jnp.transpose(back, (3, 1, 0, 2)).reshape(tokens, 3, width)
     return (dqkv, grad_new, weight_new, moment_one, moment_two)

time: 214 us -> 207 us (0.967)
  the two profiles are of different devices: /device:TPU:21 before, /device:TPU:1 now
where the time goes in v3:
time: 207 us; the launch traced here: 205 us
  starting transfers between devices  93.3 us (45%)
  waiting for transfers between devices  45.8 us (22%)
  Pallas kernels  30 us (14%)
  blocking collectives  16.7 us (8%)
  local copies, waits for them, and re-layouts  12.6 us (6%)
  other arithmetic  5.9 us (3%)
    all_to_all x4, waiting for transfers between devices, exchange(): return lax.all_to_all(array, axes, 0, 0, tiled=True)  28.6 us
    all_to_all x4, starting transfers between devices, exchange(): return lax.all_to_all(array, axes, 0, 0, tiled=True)  25.9 us
    ppermute x4, starting transfers between devices, per_device(): lax.ppermute(at(pieces, (lax.axis_index('zh') + turn) % across), DP, moves)  25.4 us
    all_to_all x1, blocking collectives, exchange(): return lax.all_to_all(array, axes, 0, 0, tiled=True)  16.7 us
    ppermute x1, starting transfers between devices, per_device(): sent = lax.ppermute(sent, 'c', SWAP)  16.1 us
    pallas_call x1, Pallas kernels, grads_call(): pl.pallas_call(grads_kernel, out_shape=jax.ShapeDtypeStruct(heads.shape,...  16 us
    ppermute x3, starting transfers between devices, per_device(): sent = lax.ppermute(sent, 'x', [(i, i ^ reach) for i in range(line)])  14.9 us
    pallas_call x1, Pallas kernels, probs_call(): pl.pallas_call(probs_kernel, out_shape=jax.ShapeDtypeStruct((length, leng...  10.8 us
  transfers between devices with their start and end apart: 15, of which 10 were waited for; matrix products, arithmetic and copies ran while one was open for 5% of the time, Pallas kernels for 13%

profile of v3, /device:TPU:1, one launch (start us, length us, event | category | flops | bytes accessed | tf_op | source)
XLA Modules:
  0.0 205.3 jit_solution(2076381370168936473)
XLA Ops:
  0.6 1.4 fusion.4
  2.0 0.1 reshape.76
  2.1 1.8 copy.17
  4.1 1.0 pad_maximum_fusion
  5.1 1.8 term.1
  6.9 16.1 %collective-permute-start = (bf16[1152,640]{1,0:T(8,128)(2,1)S(1)}, bf16[1152,640]{1,0:T(8,128)(2,1)}, u32[]{:S(2)}, u32[]{:S(2)}) collective-permute-start(bf16[1152,640]{1,0:T(8,128)(2,1)S(1)} %get-tuple-element.25), channel_id=1, source_target_pairs={{0,16},{16,0},{1,17},{17,1},{2,18},{18,2},{3,19},{19,3},{4,20},{20... | collective-permute-start | bytes 4423688 | tf_op jit(solution)/shard_map/ppermute | solution.py:323
  23.0 4.3 %all-to-all-start = ((bf16[16,224,128]{2,1,0:T(8,128)(2,1)}), bf16[16,224,128]{2,1,0:T(8,128)(2,1)}, u32[]{:S(2)}, u32[]{:S(2)}) async-start(bf16[16,224,128]{2,1,0:T(8,128)(2,1)} %pad_maximum_fusion), calls=%async_computation | async-start | bytes 1835008 | tf_op jit(solution)/shard_map/all_to_all | solution.py:288
  27.3 1.7 add_convert_fusion
  29.1 0.1 dynamic-slice_bitcast_fusion
  29.2 3.1 %collective-permute-start.1 = (bf16[576,640]{1,0:T(8,128)(2,1)S(1)}, bf16[576,640]{1,0:T(8,128)(2,1)S(1)}, u32[]{:S(2)}, u32[]{:S(2)}) collective-permute-start(bf16[576,640]{1,0:T(8,128)(2,1)S(1)} %dynamic-slice_bitcast_fusion), channel_id=1, source_target_pairs={{0,8},{8,0},{1,9},{9,1},{2,10},{10,2},{3,11},{11,3},{4,12},{12,4},... | collective-permute-start | bytes 2211848 | tf_op jit(solution)/shard_map/ppermute | solution.py:326
  32.3 2.1 %collective-permute-start.2 = (bf16[128,1152]{1,0:T(8,128)(2,1)S(1)}, bf16[128,1152]{1,0:T(8,128)(2,1)S(1)}, u32[]{:S(2)}, u32[]{:S(2)}) collective-permute-start(bf16[128,1152]{1,0:T(8,128)(2,1)S(1)} %copy-done.1), channel_id=1, source_target_pairs={{0,8},{8,0},{1,9},{9,1},{2,10},{10,2},{3,11},{11,3},{4,12},{12,4},... | collective-permute-start | bytes 884744 | tf_op jit(solution)/shard_map/ppermute | solution.py:331
  34.5 15.5 %all-to-all-done = bf16[16,224,128]{2,1,0:T(8,128)(2,1)} async-done(((bf16[16,224,128]{2,1,0:T(8,128)(2,1)}), bf16[16,224,128]{2,1,0:T(8,128)(2,1)}, u32[]{:S(2)}, u32[]{:S(2)}) %all-to-all-start) | async-done | bytes 917536 | tf_op jit(solution)/shard_map/all_to_all | solution.py:288
  50.0 0.8 slice.17
  50.8 0.6 slice.18
  51.4 1.5 reshape.80
  52.9 1.5 copy.19
  54.4 1.5 reshape.81
  55.9 0.9 collective-permute-done.1
  56.8 1.1 fusion
  57.9 5.2 %collective-permute-done.2.near_ref = bf16[128,1152]{1,0:T(8,128)(2,1)S(1)} collective-permute-done((bf16[128,1152]{1,0:T(8,128)(2,1)S(1)}, bf16[128,1152]{1,0:T(8,128)(2,1)S(1)}, u32[]{:S(2)}, u32[]{:S(2)}) %collective-permute-start.2) | collective-permute-done | bytes 294944 | tf_op jit(solution)/shard_map/ppermute | solution.py:331
  63.1 1.0 broadcast_in_dim.19
  64.1 12.9 %all-to-all-start.1 = ((bf16[32,81,128]{2,1,0:T(8,128)(2,1)}), bf16[32,81,128]{2,1,0:T(8,128)(2,1)S(1)}, u32[]{:S(2)}, u32[]{:S(2)}) async-start(bf16[32,81,128]{2,1,0:T(8,128)(2,1)} %broadcast_in_dim.19), calls=%async_computation.1 | async-start | bytes 1441792 | tf_op jit(solution)/shard_map/all_to_all | solution.py:288
  77.0 1.2 slice.16
  78.2 10.8 %probs.1.probs_ref = bf16[2048,2048]{1,0:T(8,128)(2,1)} custom-call(bf16[16,3,72,128]{3,2,1,0:T(8,128)(2,1)S(1)} %bitcast.44), custom_call_target="tpu_custom_call" | custom-call | flops 2147483648 | bytes 8388608 | tf_op jit(solution)/shard_map/probs/pallas_call | solution.py:123
  89.0 7.9 %all-to-all-done.1 = bf16[32,81,128]{2,1,0:T(8,128)(2,1)S(1)} async-done(((bf16[32,81,128]{2,1,0:T(8,128)(2,1)}), bf16[32,81,128]{2,1,0:T(8,128)(2,1)S(1)}, u32[]{:S(2)}, u32[]{:S(2)}) %all-to-all-start.1) | async-done | bytes 663584 | tf_op jit(solution)/shard_map/all_to_all | solution.py:288
  96.9 0.8 reshape.83.own_ref
  97.7 5.8 %collective-permute-start.3 = (bf16[288,1152]{1,0:T(8,128)(2,1)S(1)}, bf16[288,1152]{1,0:T(8,128)(2,1)S(1)}, u32[]{:S(2)}, u32[]{:S(2)}) collective-permute-start(bf16[288,1152]{1,0:T(8,128)(2,1)S(1)} %reshape.83.own_ref), channel_id=1, source_target_pairs={{0,16},{16,0},{1,17},{17,1},{2,18},{18,2},{3,19},{19,3},{4,20},{20... | collective-permute-start | bytes 1990664 | tf_op jit(solution)/shard_map/ppermute | solution.py:337
  103.5 1.7 collective-permute-done.3.other_ref
  105.2 1.2 project.1
  106.4 16.7 %all_to_all.25.grad_ref = bf16[16,80,128]{2,1,0:T(8,128)(2,1)S(1)} all-to-all(bf16[16,80,128]{2,1,0:T(8,128)(2,1)S(1)} %project.1), channel_id=1, replica_groups=mesh['zh'=4,'x'=8,'c'=2,'zl'=2,'y'=8] {'zl','y'}, dimensions={0} | all-to-all | bytes 655360 | tf_op jit(solution)/shard_map/all_to_all | solution.py:288
  123.1 4.6 %all-to-all-start.3 = ((bf16[8,72,640]{2,1,0:T(8,128)(2,1)}), bf16[8,72,640]{2,1,0:T(8,128)(2,1)S(1)}, u32[]{:S(2)}, u32[]{:S(2)}) async-start(bf16[8,72,640]{2,1,0:T(8,128)(2,1)} %bitcast.10), calls=%async_computation.3 | async-start | bytes 1474560 | tf_op jit(solution)/shard_map/all_to_all | solution.py:288
  127.7 16.0 %grads.1 = bf16[16,3,72,128]{3,2,1,0:T(8,128)(2,1)} custom-call(bf16[16,3,72,128]{3,2,1,0:T(8,128)(2,1)S(1)} %bitcast.45, bf16[16,80,128]{2,1,0:T(8,128)(2,1)S(1)} %all_to_all.25.grad_ref, bf16[2048,2048]{1,0:T(8,128)(2,1)} %probs.1.probs_ref), custom_call_target="tpu_custom_call" | custom-call | flops 8589934592 | bytes 8388608 | tf_op jit(solution)/shard_map/grads/pallas_call | solution.py:142
  143.7 5.2 %all-to-all-done.3.clip_ref = bf16[8,72,640]{2,1,0:T(8,128)(2,1)S(1)} async-done(((bf16[8,72,640]{2,1,0:T(8,128)(2,1)}), bf16[8,72,640]{2,1,0:T(8,128)(2,1)S(1)}, u32[]{:S(2)}, u32[]{:S(2)}) %all-to-all-start.3) | async-done | bytes 737312 | tf_op jit(solution)/shard_map/all_to_all | solution.py:288
  148.8 4.1 %all-to-all-start.4 = ((bf16[16,3,72,128]{3,2,1,0:T(8,128)(2,1)}), bf16[16,3,72,128]{3,2,1,0:T(8,128)(2,1)S(1)}, u32[]{:S(2)}, u32[]{:S(2)}) async-start(bf16[16,3,72,128]{3,2,1,0:T(8,128)(2,1)} %grads.1), calls=%async_computation.4 | async-start | bytes 1769472 | tf_op jit(solution)/shard_map/all_to_all | solution.py:288
  152.9 0.2 arrange.1
  153.1 5.7 %collective-permute-start.4 = (bf16[4,4,24,128]{3,2,1,0:T(8,128)(2,1)S(1)}, bf16[4,4,24,128]{3,2,1,0:T(8,128)(2,1)S(1)}, u32[]{:S(2)}, u32[]{:S(2)}) collective-permute-start(bf16[4,4,24,128]{3,2,1,0:T(8,128)(2,1)S(1)} %fusion.1), channel_id=1, source_target_pairs={{0,128},{32,160},{64,192},{96,224},{128,0},{160,32},{192,64},{224,... | collective-permute-start | bytes 294920 | tf_op jit(solution)/shard_map/ppermute | solution.py:353
  158.9 3.8 %collective-permute-done.4 = bf16[4,4,24,128]{3,2,1,0:T(8,128)(2,1)S(1)} collective-permute-done((bf16[4,4,24,128]{3,2,1,0:T(8,128)(2,1)S(1)}, bf16[4,4,24,128]{3,2,1,0:T(8,128)(2,1)S(1)}, u32[]{:S(2)}, u32[]{:S(2)}) %collective-permute-start.4) | collective-permute-done | bytes 98336 | tf_op jit(solution)/shard_map/ppermute | solution.py:353
  162.8 5.8 %collective-permute-start.5 = (bf16[2,4,24,128]{3,2,1,0:T(8,128)(2,1)S(1)}, bf16[2,4,24,128]{3,2,1,0:T(8,128)(2,1)S(1)}, u32[]{:S(2)}, u32[]{:S(2)}) collective-permute-start(bf16[2,4,24,128]{3,2,1,0:T(8,128)(2,1)S(1)} %fusion.2), channel_id=1, source_target_pairs={{0,64},{32,96},{64,0},{96,32},{128,192},{160,224},{192,128},{224,1... | collective-permute-start | bytes 147464 | tf_op jit(solution)/shard_map/ppermute | solution.py:353
  168.6 1.4 collective-permute-done.5
  170.1 3.3 %collective-permute-start.6 = (bf16[1,4,24,128]{3,2,1,0:T(8,128)(2,1)S(1)}, bf16[1,4,24,128]{3,2,1,0:T(8,128)(2,1)S(1)}, u32[]{:S(2)}, u32[]{:S(2)}) collective-permute-start(bf16[1,4,24,128]{3,2,1,0:T(8,128)(2,1)S(1)} %dynamic-slice_convert_fusion.2), channel_id=1, source_target_pairs={{0,32},{32,0},{64,96},{96,64},{128,160},{160,128},{192,224},{224,1... | collective-permute-start | bytes 73736 | tf_op jit(solution)/shard_map/ppermute | solution.py:353
  173.5 1.4 collective-permute-done.6
  175.0 9.5 %collective-permute-start.10 = (f32[24,128]{1,0:T(8,128)S(1)}, f32[24,128]{1,0:T(8,128)S(1)}, u32[]{:S(2)}, u32[]{:S(2)}) collective-permute-start(f32[24,128]{1,0:T(8,128)S(1)} %get-tuple-element.52), channel_id=1, source_target_pairs={{0,384},{16,896},{32,400},{48,912},{64,416},{80,928},{96,432},{112... | collective-permute-start | bytes 36872 | tf_op jit(solution)/shard_map/ppermute | solution.py:365
  184.5 3.8 %collective-permute-start.9 = (f32[24,128]{1,0:T(8,128)S(1)}, f32[24,128]{1,0:T(8,128)S(1)}, u32[]{:S(2)}, u32[]{:S(2)}) collective-permute-start(f32[24,128]{1,0:T(8,128)S(1)} %get-tuple-element.53), channel_id=1, source_target_pairs={{0,256},{16,768},{32,272},{48,784},{64,288},{80,800},{96,304},{112... | collective-permute-start | bytes 36872 | tf_op jit(solution)/shard_map/ppermute | solution.py:365
  188.2 9.8 %collective-permute-start.8 = (f32[24,128]{1,0:T(8,128)S(1)}, f32[24,128]{1,0:T(8,128)S(1)}, u32[]{:S(2)}, u32[]{:S(2)}) collective-permute-start(f32[24,128]{1,0:T(8,128)S(1)} %get-tuple-element.54), channel_id=1, source_target_pairs={{0,128},{16,640},{32,144},{48,656},{64,160},{80,672},{96,176},{112... | collective-permute-start | bytes 36872 | tf_op jit(solution)/shard_map/ppermute | solution.py:365
  198.1 2.3 %collective-permute-start.7 = (f32[24,128]{1,0:T(8,128)S(1)}, f32[24,128]{1,0:T(8,128)S(1)}, u32[]{:S(2)}, u32[]{:S(2)}) collective-permute-start(f32[24,128]{1,0:T(8,128)S(1)} %get-tuple-element.51), channel_id=1, source_target_pairs={{0,0},{16,512},{32,16},{48,528},{64,32},{80,544},{96,48},{112,560}... | collective-permute-start | bytes 36872 | tf_op jit(solution)/shard_map/ppermute | solution.py:365
  200.4 2.7 %collective-permute-done.7 = f32[24,128]{1,0:T(8,128)S(1)} collective-permute-done((f32[24,128]{1,0:T(8,128)S(1)}, f32[24,128]{1,0:T(8,128)S(1)}, u32[]{:S(2)}, u32[]{:S(2)}) %collective-permute-start.7) | collective-permute-done | bytes 12320 | tf_op jit(solution)/shard_map/ppermute | solution.py:365
  203.1 0.6 slice_add_fusion
  203.8 1.5 copy.21
  (24 shorter events, 0.3 us)
Async XLA Ops:
  4.0 1.1 copy-start
  4.0 1.1 copy-start.1
  6.9 20.4 %collective-permute-start = (bf16[1152,640]{1,0:T(8,128)(2,1)S(1)}, bf16[1152,640]{1,0:T(8,128)(2,1)}, u32[]{:S(2)}, u32[]{:S(2)}) collective-permute-start(bf16[1152,640]{1,0:T(8,128)(2,1)S(1)} %get-tuple-element.25), channel_id=1, source_target_pairs={{0,16},{16,0},{1,17},{17,1},{2,18},{18,2},{3,19},{19,3},{4,20},{20... | collective-permute-start | bytes 4423688 | tf_op jit(solution)/shard_map/ppermute | solution.py:323
  23.0 27.0 %all-to-all-start = ((bf16[16,224,128]{2,1,0:T(8,128)(2,1)}), bf16[16,224,128]{2,1,0:T(8,128)(2,1)}, u32[]{:S(2)}, u32[]{:S(2)}) async-start(bf16[16,224,128]{2,1,0:T(8,128)(2,1)} %pad_maximum_fusion), calls=%async_computation | async-start | bytes 1835008 | tf_op jit(solution)/shard_map/all_to_all | solution.py:288
  29.2 27.6 %collective-permute-start.1 = (bf16[576,640]{1,0:T(8,128)(2,1)S(1)}, bf16[576,640]{1,0:T(8,128)(2,1)S(1)}, u32[]{:S(2)}, u32[]{:S(2)}) collective-permute-start(bf16[576,640]{1,0:T(8,128)(2,1)S(1)} %dynamic-slice_bitcast_fusion), channel_id=1, source_target_pairs={{0,8},{8,0},{1,9},{9,1},{2,10},{10,2},{3,11},{11,3},{4,12},{12,4},... | collective-permute-start | bytes 2211848 | tf_op jit(solution)/shard_map/ppermute | solution.py:326
  32.3 30.8 %collective-permute-start.2 = (bf16[128,1152]{1,0:T(8,128)(2,1)S(1)}, bf16[128,1152]{1,0:T(8,128)(2,1)S(1)}, u32[]{:S(2)}, u32[]{:S(2)}) collective-permute-start(bf16[128,1152]{1,0:T(8,128)(2,1)S(1)} %copy-done.1), channel_id=1, source_target_pairs={{0,8},{8,0},{1,9},{9,1},{2,10},{10,2},{3,11},{11,3},{4,12},{12,4},... | collective-permute-start | bytes 884744 | tf_op jit(solution)/shard_map/ppermute | solution.py:331
  55.9 7.3 %copy-start.2 = (bf16[81,128]{1,0:T(8,128)(2,1)S(1)}, bf16[81,128]{1,0:T(8,128)(2,1)}, u32[]{:S(2)}) copy-start(bf16[81,128]{1,0:T(8,128)(2,1)} %reshape.81) | copy-start | bytes 62212
  64.1 32.8 %all-to-all-start.1 = ((bf16[32,81,128]{2,1,0:T(8,128)(2,1)}), bf16[32,81,128]{2,1,0:T(8,128)(2,1)S(1)}, u32[]{:S(2)}, u32[]{:S(2)}) async-start(bf16[32,81,128]{2,1,0:T(8,128)(2,1)} %broadcast_in_dim.19), calls=%async_computation.1 | async-start | bytes 1441792 | tf_op jit(solution)/shard_map/all_to_all | solution.py:288
  97.7 7.5 %collective-permute-start.3 = (bf16[288,1152]{1,0:T(8,128)(2,1)S(1)}, bf16[288,1152]{1,0:T(8,128)(2,1)S(1)}, u32[]{:S(2)}, u32[]{:S(2)}) collective-permute-start(bf16[288,1152]{1,0:T(8,128)(2,1)S(1)} %reshape.83.own_ref), channel_id=1, source_target_pairs={{0,16},{16,0},{1,17},{17,1},{2,18},{18,2},{3,19},{19,3},{4,20},{20... | collective-permute-start | bytes 1990664 | tf_op jit(solution)/shard_map/ppermute | solution.py:337
  123.1 25.8 %all-to-all-start.3 = ((bf16[8,72,640]{2,1,0:T(8,128)(2,1)}), bf16[8,72,640]{2,1,0:T(8,128)(2,1)S(1)}, u32[]{:S(2)}, u32[]{:S(2)}) async-start(bf16[8,72,640]{2,1,0:T(8,128)(2,1)} %bitcast.10), calls=%async_computation.3 | async-start | bytes 1474560 | tf_op jit(solution)/shard_map/all_to_all | solution.py:288
  148.8 54.9 %all-to-all-start.4 = ((bf16[16,3,72,128]{3,2,1,0:T(8,128)(2,1)}), bf16[16,3,72,128]{3,2,1,0:T(8,128)(2,1)S(1)}, u32[]{:S(2)}, u32[]{:S(2)}) async-start(bf16[16,3,72,128]{3,2,1,0:T(8,128)(2,1)} %grads.1), calls=%async_computation.4 | async-start | bytes 1769472 | tf_op jit(solution)/shard_map/all_to_all | solution.py:288
  153.1 9.6 %collective-permute-start.4 = (bf16[4,4,24,128]{3,2,1,0:T(8,128)(2,1)S(1)}, bf16[4,4,24,128]{3,2,1,0:T(8,128)(2,1)S(1)}, u32[]{:S(2)}, u32[]{:S(2)}) collective-permute-start(bf16[4,4,24,128]{3,2,1,0:T(8,128)(2,1)S(1)} %fusion.1), channel_id=1, source_target_pairs={{0,128},{32,160},{64,192},{96,224},{128,0},{160,32},{192,64},{224,... | collective-permute-start | bytes 294920 | tf_op jit(solution)/shard_map/ppermute | solution.py:353
  162.8 7.3 %collective-permute-start.5 = (bf16[2,4,24,128]{3,2,1,0:T(8,128)(2,1)S(1)}, bf16[2,4,24,128]{3,2,1,0:T(8,128)(2,1)S(1)}, u32[]{:S(2)}, u32[]{:S(2)}) collective-permute-start(bf16[2,4,24,128]{3,2,1,0:T(8,128)(2,1)S(1)} %fusion.2), channel_id=1, source_target_pairs={{0,64},{32,96},{64,0},{96,32},{128,192},{160,224},{192,128},{224,1... | collective-permute-start | bytes 147464 | tf_op jit(solution)/shard_map/ppermute | solution.py:353
  170.1 4.9 %collective-permute-start.6 = (bf16[1,4,24,128]{3,2,1,0:T(8,128)(2,1)S(1)}, bf16[1,4,24,128]{3,2,1,0:T(8,128)(2,1)S(1)}, u32[]{:S(2)}, u32[]{:S(2)}) collective-permute-start(bf16[1,4,24,128]{3,2,1,0:T(8,128)(2,1)S(1)} %dynamic-slice_convert_fusion.2), channel_id=1, source_target_pairs={{0,32},{32,0},{64,96},{96,64},{128,160},{160,128},{192,224},{224,1... | collective-permute-start | bytes 73736 | tf_op jit(solution)/shard_map/ppermute | solution.py:353
  175.0 25.4 %collective-permute-start.10 = (f32[24,128]{1,0:T(8,128)S(1)}, f32[24,128]{1,0:T(8,128)S(1)}, u32[]{:S(2)}, u32[]{:S(2)}) collective-permute-start(f32[24,128]{1,0:T(8,128)S(1)} %get-tuple-element.52), channel_id=1, source_target_pairs={{0,384},{16,896},{32,400},{48,912},{64,416},{80,928},{96,432},{112... | collective-permute-start | bytes 36872 | tf_op jit(solution)/shard_map/ppermute | solution.py:365
  184.5 16.0 %collective-permute-start.9 = (f32[24,128]{1,0:T(8,128)S(1)}, f32[24,128]{1,0:T(8,128)S(1)}, u32[]{:S(2)}, u32[]{:S(2)}) collective-permute-start(f32[24,128]{1,0:T(8,128)S(1)} %get-tuple-element.53), channel_id=1, source_target_pairs={{0,256},{16,768},{32,272},{48,784},{64,288},{80,800},{96,304},{112... | collective-permute-start | bytes 36872 | tf_op jit(solution)/shard_map/ppermute | solution.py:365
  188.2 12.2 %collective-permute-start.8 = (f32[24,128]{1,0:T(8,128)S(1)}, f32[24,128]{1,0:T(8,128)S(1)}, u32[]{:S(2)}, u32[]{:S(2)}) collective-permute-start(f32[24,128]{1,0:T(8,128)S(1)} %get-tuple-element.54), channel_id=1, source_target_pairs={{0,128},{16,640},{32,144},{48,656},{64,160},{80,672},{96,176},{112... | collective-permute-start | bytes 36872 | tf_op jit(solution)/shard_map/ppermute | solution.py:365
  198.1 5.0 %collective-permute-start.7 = (f32[24,128]{1,0:T(8,128)S(1)}, f32[24,128]{1,0:T(8,128)S(1)}, u32[]{:S(2)}, u32[]{:S(2)}) collective-permute-start(f32[24,128]{1,0:T(8,128)S(1)} %get-tuple-element.51), channel_id=1, source_target_pairs={{0,0},{16,512},{32,16},{48,528},{64,32},{80,544},{96,48},{112,560}... | collective-permute-start | bytes 36872 | tf_op jit(solution)/shard_map/ppermute | solution.py:365

commit v4 on v3

--- a/solution.py
+++ b/solution.py
@@ -248,31 +248,40 @@
     )(core, own, other, dout, near)
 
 
-def arrange_kernel(clip_ref, out_ref):
-    line, across = out_ref.shape[0], out_ref.shape[1]
+def arrange_kernel(clip_ref, out_ref, blocks_ref):
+    line, across, high = blocks_ref.shape[0], blocks_ref.shape[1], blocks_ref.shape[2]
     cols = clip_ref.shape[1]
-    total = clip_ref[0].astype(jnp.float32)
-    for s in range(1, clip_ref.shape[0]):
-        total = total + clip_ref[s].astype(jnp.float32)
-    turned = total.T
-    out_ref[...] = jnp.zeros_like(out_ref)
+    turned = clip_ref[0].T
+    blocks_ref[...] = jnp.zeros_like(blocks_ref)
     for z in range(across):
         for x in range(line):
             start = (z * line + x) * ROWS_DEV
-            out_ref[x, z, :ROWS_DEV, :cols] = turned[start : start + ROWS_DEV]
+            blocks_ref[x, z, :ROWS_DEV, :cols] = turned[start : start + ROWS_DEV]
+    for z in range(across):
+        out_ref[:, z * high : (z + 1) * high, :] = blocks_ref[:, z].astype(jnp.bfloat16)
 
 
 def arrange_call(clip, line, across):
     vmem = pl.BlockSpec(memory_space=pltpu.VMEM)
     return pl.pallas_call(
         arrange_kernel,
-        out_shape=jax.ShapeDtypeStruct((line, across, 24, LANES), jnp.float32),
+        out_shape=jax.ShapeDtypeStruct((line, across * 24, LANES), jnp.bfloat16),
         in_specs=[vmem],
         out_specs=vmem,
+        scratch_shapes=[pltpu.VMEM((line, across, 24, LANES), jnp.float32)],
         compiler_params=pltpu.CompilerParams(vmem_limit_bytes=16 * 2**20),
         cost_estimate=pl.CostEstimate(flops=0, transcendentals=0, bytes_accessed=0),
         name="arrange",
     )(clip)
+
+
+def halve(pieces, axis, turn):
+    bit = (lax.axis_index(axis) >> turn) % 2
+    pairs = pieces.reshape((pieces.shape[0] // 2, 2) + pieces.shape[1:])
+    moves = [(i, i ^ (1 << turn)) for i in range(lax.axis_size(axis))]
+    sent = lax.dynamic_index_in_dim(pairs, 1 - bit, 1, keepdims=False).astype(jnp.bfloat16)
+    kept = lax.dynamic_index_in_dim(pairs, bit, 1, keepdims=False)
+    return kept.astype(jnp.float32) + lax.ppermute(sent, axis, moves).astype(jnp.float32)
 
 
 SEQ = ("zl", "y")
@@ -329,31 +338,31 @@
     lane = math.gcd(SHARE * width, LANES)
     row_block = jnp.transpose(columns, (1, 0, 2)).reshape(SHARE * width // lane, lane)
     near = lax.ppermute(dout, "zl", SWAP)
-    row_block, quad, near = lax.optimization_barrier((row_block, quad, near))
+    row_block, quad = lax.optimization_barrier((row_block, quad))
     own = exchange(jnp.broadcast_to(row_block[None], (row_count,) + row_block.shape), ROWS)
     probs = probs_call(heads_qkv)
-    own, probs, near = lax.optimization_barrier((own, probs, near))
+    clip = halve(quad.reshape(ring, cols, quad.shape[1]), "y", 0)
+    own, probs, near, clip = lax.optimization_barrier((own, probs, near, clip))
     own = own.reshape(row_count * SHARE, width)
     other = lax.ppermute(own, "c", SWAP)
     grad_rows = project_call(core_id, own, other, dout, near, seq_count)
     heads_grad = exchange(grad_rows, SEQ)
 
-    quad, heads_grad, probs = lax.optimization_barrier((quad, heads_grad, probs))
-    clip = exchange(quad.reshape(ring, cols, quad.shape[1]), "y")
+    line, across = lax.axis_size("x"), lax.axis_size("zh")
+    clip, _ = lax.optimization_barrier((clip, grad_rows))
+    step = lax.axis_index("y") // 2
+    total = at(clip, step)
+    for turn in range(1, ring // 2):
+        moves = [(i, (i + 2 * turn) % ring) for i in range(ring)]
+        sent = lax.ppermute(at(clip, (step + turn) % (ring // 2)).astype(jnp.bfloat16), "y", moves)
+        total = total + sent.astype(jnp.float32)
+    pieces = arrange_call(total[None], line, across)
+    pieces, heads_grad, probs = lax.optimization_barrier((pieces, heads_grad, probs))
+    pieces = exchange(pieces, "x")
     local = grads_call(heads_qkv, heads_grad, probs)
-    local, clip = lax.optimization_barrier((local, clip))
-
-    line, across = lax.axis_size("x"), lax.axis_size("zh")
-    pieces = arrange_call(clip, line, across)
-    reach = line // 2
-    while reach:
-        bit = (lax.axis_index("x") // reach) % 2
-        halves = pieces.reshape((2, reach) + pieces.shape[1:])
-        sent = at(halves, 1 - bit).astype(jnp.bfloat16)
-        sent = lax.ppermute(sent, "x", [(i, i ^ reach) for i in range(line)])
-        pieces = at(halves, bit) + sent.astype(jnp.float32)
-        reach //= 2
-    pieces = pieces[0]
+    local, pieces = lax.optimization_barrier((local, pieces))
+
+    pieces = jnp.sum(pieces.astype(jnp.float32), axis=0).reshape(across, 24, LANES)
     grad_new = jnp.zeros((24, LANES), jnp.float32)
     for turn in range(across):
         moves = [

time: 207 us -> 194 us (0.937); the launches traced: 205 us -> 190 us
  blocking collectives: 16.7 us -> 0 us
  starting transfers between devices: 93.3 us -> 102 us
  waiting for transfers between devices: 45.8 us -> 40.3 us
  local copies, waits for them, and re-layouts: 12.6 us -> 9.01 us
    all_to_all x1 -> x0, blocking collectives: 16.7 us -> none  [exchange(): return lax.all_to_all(array, axes, 0, 0, tiled=True)]
    all_to_all x4 -> x5, waiting for transfers between devices: 28.6 us -> 17.7 us  [exchange(): return lax.all_to_all(array, axes, 0, 0, tiled=True)]
    all_to_all x4 -> x5, starting transfers between devices: 25.9 us -> 35.3 us  [exchange(): return lax.all_to_all(array, axes, 0, 0, tiled=True)]
    ppermute x1, waiting for transfers between devices: 0.94 us -> 5.74 us  [per_device(): sent = lax.ppermute(at(pair, 1 - side), 'zl', SWAP)]
    ppermute x3 -> x4, starting transfers between devices: 14.9 us -> 17.8 us  [the longest x3 14.5 us: per_device(): lax.ppermute(at(clip, (step + turn) % (ring // 2)).astype(jnp.bfloat16),...]
    ppermute x1, starting transfers between devices: 5.8 us -> 2.99 us  [per_device(): other = lax.ppermute(own, 'c', SWAP)]
    ppermute x3 -> x4, waiting for transfers between devices: 6.67 us -> 5.27 us  [the longest x3 5.27 us: per_device(): lax.ppermute(at(clip, (step + turn) % (ring // 2)).astype(jnp.bfloat16),...]
  transfers between devices with their start and end apart: 15 -> 17, of which waited for: 10 -> 7; matrix products, arithmetic and copies ran while one was open for 5% -> 3% of each run, Pallas kernels for 13% -> 15%
where the time goes in v4:
time: 194 us; the launch traced here: 190 us
  starting transfers between devices  102 us (53%)
  waiting for transfers between devices  40.3 us (21%)
  Pallas kernels  31.5 us (16%)
  local copies, waits for them, and re-layouts  9.01 us (5%)
  other arithmetic  5.92 us (3%)
    all_to_all x5, starting transfers between devices, exchange(): return lax.all_to_all(array, axes, 0, 0, tiled=True)  35.3 us
    ppermute x4, starting transfers between devices, per_device(): lax.ppermute(at(pieces, (lax.axis_index('zh') + turn) % across), DP, moves)  23.6 us
    all_to_all x5, waiting for transfers between devices, exchange(): return lax.all_to_all(array, axes, 0, 0, tiled=True)  17.7 us
    ppermute x1, starting transfers between devices, per_device(): sent = lax.ppermute(sent, 'c', SWAP)  16.1 us
    pallas_call x1, Pallas kernels, grads_call(): pl.pallas_call(grads_kernel, out_shape=jax.ShapeDtypeStruct(heads.shape,...  16 us
    ppermute x3, starting transfers between devices, per_device(): lax.ppermute(at(clip, (step + turn) % (ring // 2)).astype(jnp.bfloat16),...  14.5 us
    pallas_call x1, Pallas kernels, probs_call(): pl.pallas_call(probs_kernel, out_shape=jax.ShapeDtypeStruct((length, leng...  10.8 us
    ppermute x1, waiting for transfers between devices, per_device(): sent = lax.ppermute(at(pair, 1 - side), 'zl', SWAP)  5.74 us
  transfers between devices with their start and end apart: 17, of which 7 were waited for; matrix products, arithmetic and copies ran while one was open for 3% of the time, Pallas kernels for 15%

profile of v4, /device:TPU:1, one launch (start us, length us, event | category | flops | bytes accessed | tf_op | source)
XLA Modules:
  0.0 190.1 jit_solution(6954574164690444905)
XLA Ops:
  0.6 1.4 fusion.8
  2.0 0.1 reshape.58
  2.1 1.8 copy.18
  4.0 0.0 copy-start
  4.0 0.1 copy.19
  4.1 1.0 pad_maximum_fusion
  5.1 1.8 term.1
  6.9 16.1 %collective-permute-start = (bf16[1152,640]{1,0:T(8,128)(2,1)S(1)}, bf16[1152,640]{1,0:T(8,128)(2,1)}, u32[]{:S(2)}, u32[]{:S(2)}) collective-permute-start(bf16[1152,640]{1,0:T(8,128)(2,1)S(1)} %get-tuple-element.26), channel_id=1, source_target_pairs={{0,16},{16,0},{1,17},{17,1},{2,18},{18,2},{3,19},{19,3},{4,20},{20... | collective-permute-start | bytes 4423688 | tf_op jit(solution)/shard_map/ppermute | solution.py:332
  23.0 4.3 %all-to-all-start = ((bf16[16,224,128]{2,1,0:T(8,128)(2,1)}), bf16[16,224,128]{2,1,0:T(8,128)(2,1)}, u32[]{:S(2)}, u32[]{:S(2)}) async-start(bf16[16,224,128]{2,1,0:T(8,128)(2,1)} %pad_maximum_fusion), calls=%async_computation | async-start | bytes 1835008 | tf_op jit(solution)/shard_map/all_to_all | solution.py:297
  27.3 1.7 add_convert_fusion
  29.1 0.1 dynamic-slice_bitcast_fusion
  29.2 3.1 %collective-permute-start.1 = (bf16[576,640]{1,0:T(8,128)(2,1)S(1)}, bf16[576,640]{1,0:T(8,128)(2,1)S(1)}, u32[]{:S(2)}, u32[]{:S(2)}) collective-permute-start(bf16[576,640]{1,0:T(8,128)(2,1)S(1)} %dynamic-slice_bitcast_fusion), channel_id=1, source_target_pairs={{0,8},{8,0},{1,9},{9,1},{2,10},{10,2},{3,11},{11,3},{4,12},{12,4},... | collective-permute-start | bytes 2211848 | tf_op jit(solution)/shard_map/ppermute | solution.py:335
  32.3 17.7 %all-to-all-done = bf16[16,224,128]{2,1,0:T(8,128)(2,1)} async-done(((bf16[16,224,128]{2,1,0:T(8,128)(2,1)}), bf16[16,224,128]{2,1,0:T(8,128)(2,1)}, u32[]{:S(2)}, u32[]{:S(2)}) %all-to-all-start) | async-done | bytes 917536 | tf_op jit(solution)/shard_map/all_to_all | solution.py:297
  50.0 0.8 slice.17
  50.8 0.1 reshape.62
  50.9 0.1 reshape.63
  51.1 5.7 %collective-permute-done.1 = bf16[576,640]{1,0:T(8,128)(2,1)S(1)} collective-permute-done((bf16[576,640]{1,0:T(8,128)(2,1)S(1)}, bf16[576,640]{1,0:T(8,128)(2,1)S(1)}, u32[]{:S(2)}, u32[]{:S(2)}) %collective-permute-start.1) | collective-permute-done | bytes 737312 | tf_op jit(solution)/shard_map/ppermute | solution.py:335
  56.8 0.2 fusion
  57.0 1.1 broadcast_in_dim.22
  58.1 13.0 %all-to-all-start.1 = ((bf16[32,81,128]{2,1,0:T(8,128)(2,1)}), bf16[32,81,128]{2,1,0:T(8,128)(2,1)}, u32[]{:S(2)}, u32[]{:S(2)}) async-start(bf16[32,81,128]{2,1,0:T(8,128)(2,1)} %broadcast_in_dim.22), calls=%async_computation.1 | async-start | bytes 1441792 | tf_op jit(solution)/shard_map/all_to_all | solution.py:297
  71.1 3.3 %collective-permute-start.3 = (bf16[4,72,640]{2,1,0:T(8,128)(2,1)S(1)}, bf16[4,72,640]{2,1,0:T(8,128)(2,1)S(1)}, u32[]{:S(2)}, u32[]{:S(2)}) collective-permute-start(bf16[4,72,640]{2,1,0:T(8,128)(2,1)S(1)} %dynamic-slice_bitcast_fusion.1), channel_id=1, source_target_pairs={{0,1},{1,0},{2,3},{3,2},{4,5},{5,4},{6,7},{7,6},{8,9},{9,8},{10,11... | collective-permute-start | bytes 1105928 | tf_op jit(solution)/shard_map/ppermute | solution.py:284
  74.5 3.2 %collective-permute-start.2 = (bf16[128,1152]{1,0:T(8,128)(2,1)S(1)}, bf16[128,1152]{1,0:T(8,128)(2,1)S(1)}, u32[]{:S(2)}, u32[]{:S(2)}) collective-permute-start(bf16[128,1152]{1,0:T(8,128)(2,1)S(1)} %copy-done.1), channel_id=1, source_target_pairs={{0,8},{8,0},{1,9},{9,1},{2,10},{10,2},{3,11},{11,3},{4,12},{12,4},... | collective-permute-start | bytes 884744 | tf_op jit(solution)/shard_map/ppermute | solution.py:340
  77.7 1.2 slice.16
  79.0 10.8 %probs.1.probs_ref = bf16[2048,2048]{1,0:T(8,128)(2,1)} custom-call(bf16[16,3,72,128]{3,2,1,0:T(8,128)(2,1)S(1)} %bitcast.58), custom_call_target="tpu_custom_call" | custom-call | flops 2147483648 | bytes 8388608 | tf_op jit(solution)/shard_map/probs/pallas_call | solution.py:123
  89.8 0.9 convert_add_fusion.1
  90.7 5.6 %collective-permute-done.2.near_ref = bf16[128,1152]{1,0:T(8,128)(2,1)S(1)} collective-permute-done((bf16[128,1152]{1,0:T(8,128)(2,1)S(1)}, bf16[128,1152]{1,0:T(8,128)(2,1)S(1)}, u32[]{:S(2)}, u32[]{:S(2)}) %collective-permute-start.2) | collective-permute-done | bytes 294944 | tf_op jit(solution)/shard_map/ppermute | solution.py:340
  96.3 1.9 reshape.65.own_ref
  98.2 3.0 %collective-permute-start.4 = (bf16[288,1152]{1,0:T(8,128)(2,1)S(1)}, bf16[288,1152]{1,0:T(8,128)(2,1)S(1)}, u32[]{:S(2)}, u32[]{:S(2)}) collective-permute-start(bf16[288,1152]{1,0:T(8,128)(2,1)S(1)} %reshape.65.own_ref), channel_id=1, source_target_pairs={{0,16},{16,0},{1,17},{17,1},{2,18},{18,2},{3,19},{19,3},{4,20},{20... | collective-permute-start | bytes 1990664 | tf_op jit(solution)/shard_map/ppermute | solution.py:347
  101.2 1.7 collective-permute-done.4.other_ref
  102.9 2.0 %project.1 = bf16[16,80,128]{2,1,0:T(8,128)(2,1)} custom-call(s32[1]{0:T(128)} %bitcast.6.refs_0_.core_ref, bf16[288,1152]{1,0:T(8,128)(2,1)S(1)} %reshape.65.own_ref, bf16[288,1152]{1,0:T(8,128)(2,1)S(1)} %collective-permute-done.4.other_ref, bf16[128,1152]{1,0:T(8,128)(2,1)S(1)} %copy-done.1, bf16[128,1152]{1,0:T(8,128)(2,1)S(1)} %collective-permute-done.2.near_ref), custom_call_target="tpu_custom_call" | custom-call | flops 679477248 | bytes 5308416 | tf_op jit(solution)/shard_map/project/pallas_call | solution.py:237
  104.9 6.6 %all-to-all-start.2 = ((bf16[16,80,128]{2,1,0:T(8,128)(2,1)}), bf16[16,80,128]{2,1,0:T(8,128)(2,1)S(1)}, u32[]{:S(2)}, u32[]{:S(2)}) async-start(bf16[16,80,128]{2,1,0:T(8,128)(2,1)} %project.1), calls=%async_computation.2 | async-start | bytes 655360 | tf_op jit(solution)/shard_map/all_to_all | solution.py:297
  111.6 4.1 %collective-permute-start.5 = (bf16[72,640]{1,0:T(8,128)(2,1)S(1)}, bf16[72,640]{1,0:T(8,128)(2,1)S(1)}, u32[]{:S(2)}, u32[]{:S(2)}) collective-permute-start(bf16[72,640]{1,0:T(8,128)(2,1)S(1)} %get-tuple-element.53), channel_id=1, source_target_pairs={{0,2},{1,3},{2,4},{3,5},{4,6},{5,7},{6,0},{7,1},{8,10},{9,11},{10,... | collective-permute-start | bytes 276488 | tf_op jit(solution)/shard_map/ppermute | solution.py:357
  115.7 5.2 %collective-permute-start.6 = (bf16[72,640]{1,0:T(8,128)(2,1)S(1)}, bf16[72,640]{1,0:T(8,128)(2,1)S(1)}, u32[]{:S(2)}, u32[]{:S(2)}) collective-permute-start(bf16[72,640]{1,0:T(8,128)(2,1)S(1)} %get-tuple-element.55), channel_id=1, source_target_pairs={{0,4},{1,5},{2,6},{3,7},{4,0},{5,1},{6,2},{7,3},{8,12},{9,13},{10,... | collective-permute-start | bytes 276488 | tf_op jit(solution)/shard_map/ppermute | solution.py:357
  120.9 5.2 %collective-permute-start.7 = (bf16[72,640]{1,0:T(8,128)(2,1)S(1)}, bf16[72,640]{1,0:T(8,128)(2,1)S(1)}, u32[]{:S(2)}, u32[]{:S(2)}) collective-permute-start(bf16[72,640]{1,0:T(8,128)(2,1)S(1)} %get-tuple-element.54), channel_id=1, source_target_pairs={{0,6},{1,7},{2,0},{3,1},{4,2},{5,3},{6,4},{7,5},{8,14},{9,15},{10,... | collective-permute-start | bytes 276488 | tf_op jit(solution)/shard_map/ppermute | solution.py:357
  126.1 4.5 %collective-permute-done.6 = bf16[72,640]{1,0:T(8,128)(2,1)S(1)} collective-permute-done((bf16[72,640]{1,0:T(8,128)(2,1)S(1)}, bf16[72,640]{1,0:T(8,128)(2,1)S(1)}, u32[]{:S(2)}, u32[]{:S(2)}) %collective-permute-start.6) | collective-permute-done | bytes 92192 | tf_op jit(solution)/shard_map/ppermute | solution.py:357
  130.6 0.8 collective-permute-done.7
  131.5 0.9 arrange.1
  132.4 5.2 %all-to-all-start.3 = ((bf16[8,96,128]{2,1,0:T(8,128)(2,1)}), bf16[8,96,128]{2,1,0:T(8,128)(2,1)S(1)}, u32[]{:S(2)}, u32[]{:S(2)}) async-start(bf16[8,96,128]{2,1,0:T(8,128)(2,1)} %arrange.1), calls=%async_computation.3 | async-start | bytes 393216 | tf_op jit(solution)/shard_map/all_to_all | solution.py:297
  137.6 16.0 %grads.1 = bf16[16,3,72,128]{3,2,1,0:T(8,128)(2,1)} custom-call(bf16[16,3,72,128]{3,2,1,0:T(8,128)(2,1)S(1)} %bitcast.59, bf16[16,80,128]{2,1,0:T(8,128)(2,1)S(1)} %all-to-all-done.2.grad_ref, bf16[2048,2048]{1,0:T(8,128)(2,1)} %probs.1.probs_ref), custom_call_target="tpu_custom_call" | custom-call | flops 8589934592 | bytes 8388608 | tf_op jit(solution)/shard_map/grads/pallas_call | solution.py:142
  153.5 6.2 %all-to-all-start.4 = ((bf16[16,3,72,128]{3,2,1,0:T(8,128)(2,1)}), bf16[16,3,72,128]{3,2,1,0:T(8,128)(2,1)S(1)}, u32[]{:S(2)}, u32[]{:S(2)}) async-start(bf16[16,3,72,128]{3,2,1,0:T(8,128)(2,1)} %grads.1), calls=%async_computation.4 | async-start | bytes 1769472 | tf_op jit(solution)/shard_map/all_to_all | solution.py:297
  159.9 6.0 %collective-permute-start.10 = (f32[24,128]{1,0:T(8,128)S(1)}, f32[24,128]{1,0:T(8,128)S(1)}, u32[]{:S(2)}, u32[]{:S(2)}) collective-permute-start(f32[24,128]{1,0:T(8,128)S(1)} %get-tuple-element.58), channel_id=1, source_target_pairs={{0,256},{16,768},{32,272},{48,784},{64,288},{80,800},{96,304},{112... | collective-permute-start | bytes 36872 | tf_op jit(solution)/shard_map/ppermute | solution.py:374
  165.8 8.0 %collective-permute-start.11 = (f32[24,128]{1,0:T(8,128)S(1)}, f32[24,128]{1,0:T(8,128)S(1)}, u32[]{:S(2)}, u32[]{:S(2)}) collective-permute-start(f32[24,128]{1,0:T(8,128)S(1)} %get-tuple-element.57), channel_id=1, source_target_pairs={{0,384},{16,896},{32,400},{48,912},{64,416},{80,928},{96,432},{112... | collective-permute-start | bytes 36872 | tf_op jit(solution)/shard_map/ppermute | solution.py:374
  173.8 6.0 %collective-permute-start.8 = (f32[24,128]{1,0:T(8,128)S(1)}, f32[24,128]{1,0:T(8,128)S(1)}, u32[]{:S(2)}, u32[]{:S(2)}) collective-permute-start(f32[24,128]{1,0:T(8,128)S(1)} %get-tuple-element.56), channel_id=1, source_target_pairs={{0,0},{16,512},{32,16},{48,528},{64,32},{80,544},{96,48},{112,560}... | collective-permute-start | bytes 36872 | tf_op jit(solution)/shard_map/ppermute | solution.py:374
  179.8 3.7 %collective-permute-start.9 = (f32[24,128]{1,0:T(8,128)S(1)}, f32[24,128]{1,0:T(8,128)S(1)}, u32[]{:S(2)}, u32[]{:S(2)}) collective-permute-start(f32[24,128]{1,0:T(8,128)S(1)} %get-tuple-element.59), channel_id=1, source_target_pairs={{0,128},{16,640},{32,144},{48,656},{64,160},{80,672},{96,176},{112... | collective-permute-start | bytes 36872 | tf_op jit(solution)/shard_map/ppermute | solution.py:374
  183.6 4.3 %collective-permute-done.9 = f32[24,128]{1,0:T(8,128)S(1)} collective-permute-done((f32[24,128]{1,0:T(8,128)S(1)}, f32[24,128]{1,0:T(8,128)S(1)}, u32[]{:S(2)}, u32[]{:S(2)}) %collective-permute-start.9) | collective-permute-done | bytes 12320 | tf_op jit(solution)/shard_map/ppermute | solution.py:374
  187.8 0.6 slice_add_fusion
  188.4 0.1 copy.22
  188.5 1.5 copy.23
  (30 shorter events, 0.3 us)
Async XLA Ops:
  4.0 1.1 copy-start
  4.0 1.1 copy-start.1
  6.9 20.4 %collective-permute-start = (bf16[1152,640]{1,0:T(8,128)(2,1)S(1)}, bf16[1152,640]{1,0:T(8,128)(2,1)}, u32[]{:S(2)}, u32[]{:S(2)}) collective-permute-start(bf16[1152,640]{1,0:T(8,128)(2,1)S(1)} %get-tuple-element.26), channel_id=1, source_target_pairs={{0,16},{16,0},{1,17},{17,1},{2,18},{18,2},{3,19},{19,3},{4,20},{20... | collective-permute-start | bytes 4423688 | tf_op jit(solution)/shard_map/ppermute | solution.py:332
  23.0 27.0 %all-to-all-start = ((bf16[16,224,128]{2,1,0:T(8,128)(2,1)}), bf16[16,224,128]{2,1,0:T(8,128)(2,1)}, u32[]{:S(2)}, u32[]{:S(2)}) async-start(bf16[16,224,128]{2,1,0:T(8,128)(2,1)} %pad_maximum_fusion), calls=%async_computation | async-start | bytes 1835008 | tf_op jit(solution)/shard_map/all_to_all | solution.py:297
  29.2 27.6 %collective-permute-start.1 = (bf16[576,640]{1,0:T(8,128)(2,1)S(1)}, bf16[576,640]{1,0:T(8,128)(2,1)S(1)}, u32[]{:S(2)}, u32[]{:S(2)}) collective-permute-start(bf16[576,640]{1,0:T(8,128)(2,1)S(1)} %dynamic-slice_bitcast_fusion), channel_id=1, source_target_pairs={{0,8},{8,0},{1,9},{9,1},{2,10},{10,2},{3,11},{11,3},{4,12},{12,4},... | collective-permute-start | bytes 2211848 | tf_op jit(solution)/shard_map/ppermute | solution.py:335
  57.0 14.1 %copy-start.2 = (bf16[576,640]{1,0:T(8,128)(2,1)}, bf16[576,640]{1,0:T(8,128)(2,1)S(1)}, u32[]{:S(2)}) copy-start(bf16[576,640]{1,0:T(8,128)(2,1)S(1)} %fusion) | copy-start | bytes 2211844
  58.1 38.3 %all-to-all-start.1 = ((bf16[32,81,128]{2,1,0:T(8,128)(2,1)}), bf16[32,81,128]{2,1,0:T(8,128)(2,1)}, u32[]{:S(2)}, u32[]{:S(2)}) async-start(bf16[32,81,128]{2,1,0:T(8,128)(2,1)} %broadcast_in_dim.22), calls=%async_computation.1 | async-start | bytes 1441792 | tf_op jit(solution)/shard_map/all_to_all | solution.py:297
  71.1 18.6 %collective-permute-start.3 = (bf16[4,72,640]{2,1,0:T(8,128)(2,1)S(1)}, bf16[4,72,640]{2,1,0:T(8,128)(2,1)S(1)}, u32[]{:S(2)}, u32[]{:S(2)}) collective-permute-start(bf16[4,72,640]{2,1,0:T(8,128)(2,1)S(1)} %dynamic-slice_bitcast_fusion.1), channel_id=1, source_target_pairs={{0,1},{1,0},{2,3},{3,2},{4,5},{5,4},{6,7},{7,6},{8,9},{9,8},{10,11... | collective-permute-start | bytes 1105928 | tf_op jit(solution)/shard_map/ppermute | solution.py:284
  74.5 21.9 %collective-permute-start.2 = (bf16[128,1152]{1,0:T(8,128)(2,1)S(1)}, bf16[128,1152]{1,0:T(8,128)(2,1)S(1)}, u32[]{:S(2)}, u32[]{:S(2)}) collective-permute-start(bf16[128,1152]{1,0:T(8,128)(2,1)S(1)} %copy-done.1), channel_id=1, source_target_pairs={{0,8},{8,0},{1,9},{9,1},{2,10},{10,2},{3,11},{11,3},{4,12},{12,4},... | collective-permute-start | bytes 884744 | tf_op jit(solution)/shard_map/ppermute | solution.py:340
  78.9 10.8 %copy-start.3 = (bf16[576,640]{1,0:T(8,128)(2,1)S(1)}, bf16[576,640]{1,0:T(8,128)(2,1)}, u32[]{:S(2)}) copy-start(bf16[576,640]{1,0:T(8,128)(2,1)} %copy-done.2) | copy-start | bytes 2211844
  98.2 13.3 %copy-start.4 = (f32[4,72,640]{2,1,0:T(8,128)S(1)}, f32[4,72,640]{2,1,0:T(8,128)}, u32[]{:S(2)}) copy-start(f32[4,72,640]{2,1,0:T(8,128)} %convert_add_fusion.1) | copy-start | bytes 2211844
  98.2 4.7 %collective-permute-start.4 = (bf16[288,1152]{1,0:T(8,128)(2,1)S(1)}, bf16[288,1152]{1,0:T(8,128)(2,1)S(1)}, u32[]{:S(2)}, u32[]{:S(2)}) collective-permute-start(bf16[288,1152]{1,0:T(8,128)(2,1)S(1)} %reshape.65.own_ref), channel_id=1, source_target_pairs={{0,16},{16,0},{1,17},{17,1},{2,18},{18,2},{3,19},{19,3},{4,20},{20... | collective-permute-start | bytes 1990664 | tf_op jit(solution)/shard_map/ppermute | solution.py:347
  104.9 27.5 %all-to-all-start.2 = ((bf16[16,80,128]{2,1,0:T(8,128)(2,1)}), bf16[16,80,128]{2,1,0:T(8,128)(2,1)S(1)}, u32[]{:S(2)}, u32[]{:S(2)}) async-start(bf16[16,80,128]{2,1,0:T(8,128)(2,1)} %project.1), calls=%async_computation.2 | async-start | bytes 655360 | tf_op jit(solution)/shard_map/all_to_all | solution.py:297
  111.6 14.5 %collective-permute-start.5 = (bf16[72,640]{1,0:T(8,128)(2,1)S(1)}, bf16[72,640]{1,0:T(8,128)(2,1)S(1)}, u32[]{:S(2)}, u32[]{:S(2)}) collective-permute-start(bf16[72,640]{1,0:T(8,128)(2,1)S(1)} %get-tuple-element.53), channel_id=1, source_target_pairs={{0,2},{1,3},{2,4},{3,5},{4,6},{5,7},{6,0},{7,1},{8,10},{9,11},{10,... | collective-permute-start | bytes 276488 | tf_op jit(solution)/shard_map/ppermute | solution.py:357
  115.7 14.9 %collective-permute-start.6 = (bf16[72,640]{1,0:T(8,128)(2,1)S(1)}, bf16[72,640]{1,0:T(8,128)(2,1)S(1)}, u32[]{:S(2)}, u32[]{:S(2)}) collective-permute-start(bf16[72,640]{1,0:T(8,128)(2,1)S(1)} %get-tuple-element.55), channel_id=1, source_target_pairs={{0,4},{1,5},{2,6},{3,7},{4,0},{5,1},{6,2},{7,3},{8,12},{9,13},{10,... | collective-permute-start | bytes 276488 | tf_op jit(solution)/shard_map/ppermute | solution.py:357
  120.9 10.5 %collective-permute-start.7 = (bf16[72,640]{1,0:T(8,128)(2,1)S(1)}, bf16[72,640]{1,0:T(8,128)(2,1)S(1)}, u32[]{:S(2)}, u32[]{:S(2)}) collective-permute-start(bf16[72,640]{1,0:T(8,128)(2,1)S(1)} %get-tuple-element.54), channel_id=1, source_target_pairs={{0,6},{1,7},{2,0},{3,1},{4,2},{5,3},{6,4},{7,5},{8,14},{9,15},{10,... | collective-permute-start | bytes 276488 | tf_op jit(solution)/shard_map/ppermute | solution.py:357
  132.4 21.2 %all-to-all-start.3 = ((bf16[8,96,128]{2,1,0:T(8,128)(2,1)}), bf16[8,96,128]{2,1,0:T(8,128)(2,1)S(1)}, u32[]{:S(2)}, u32[]{:S(2)}) async-start(bf16[8,96,128]{2,1,0:T(8,128)(2,1)} %arrange.1), calls=%async_computation.3 | async-start | bytes 393216 | tf_op jit(solution)/shard_map/all_to_all | solution.py:297
  153.5 34.9 %all-to-all-start.4 = ((bf16[16,3,72,128]{3,2,1,0:T(8,128)(2,1)}), bf16[16,3,72,128]{3,2,1,0:T(8,128)(2,1)S(1)}, u32[]{:S(2)}, u32[]{:S(2)}) async-start(bf16[16,3,72,128]{3,2,1,0:T(8,128)(2,1)} %grads.1), calls=%async_computation.4 | async-start | bytes 1769472 | tf_op jit(solution)/shard_map/all_to_all | solution.py:297
  159.9 23.7 %collective-permute-start.10 = (f32[24,128]{1,0:T(8,128)S(1)}, f32[24,128]{1,0:T(8,128)S(1)}, u32[]{:S(2)}, u32[]{:S(2)}) collective-permute-start(f32[24,128]{1,0:T(8,128)S(1)} %get-tuple-element.58), channel_id=1, source_target_pairs={{0,256},{16,768},{32,272},{48,784},{64,288},{80,800},{96,304},{112... | collective-permute-start | bytes 36872 | tf_op jit(solution)/shard_map/ppermute | solution.py:374
  165.8 17.7 %collective-permute-start.11 = (f32[24,128]{1,0:T(8,128)S(1)}, f32[24,128]{1,0:T(8,128)S(1)}, u32[]{:S(2)}, u32[]{:S(2)}) collective-permute-start(f32[24,128]{1,0:T(8,128)S(1)} %get-tuple-element.57), channel_id=1, source_target_pairs={{0,384},{16,896},{32,400},{48,912},{64,416},{80,928},{96,432},{112... | collective-permute-start | bytes 36872 | tf_op jit(solution)/shard_map/ppermute | solution.py:374
  173.8 9.7 %collective-permute-start.8 = (f32[24,128]{1,0:T(8,128)S(1)}, f32[24,128]{1,0:T(8,128)S(1)}, u32[]{:S(2)}, u32[]{:S(2)}) collective-permute-start(f32[24,128]{1,0:T(8,128)S(1)} %get-tuple-element.56), channel_id=1, source_target_pairs={{0,0},{16,512},{32,16},{48,528},{64,32},{80,544},{96,48},{112,560}... | collective-permute-start | bytes 36872 | tf_op jit(solution)/shard_map/ppermute | solution.py:374
  179.8 8.0 %collective-permute-start.9 = (f32[24,128]{1,0:T(8,128)S(1)}, f32[24,128]{1,0:T(8,128)S(1)}, u32[]{:S(2)}, u32[]{:S(2)}) collective-permute-start(f32[24,128]{1,0:T(8,128)S(1)} %get-tuple-element.59), channel_id=1, source_target_pairs={{0,128},{16,640},{32,144},{48,656},{64,160},{80,672},{96,176},{112... | collective-permute-start | bytes 36872 | tf_op jit(solution)/shard_map/ppermute | solution.py:374

commit v5 on v4

--- a/solution.py
+++ b/solution.py
@@ -8,7 +8,7 @@
 from jax.sharding import Mesh, PartitionSpec as P
 
 HD = 72
-BLOCK = 256
+BLOCK = 512
 
 BETA_ONE = 0.9
 BETA_TWO = 0.999
@@ -251,7 +251,10 @@
 def arrange_kernel(clip_ref, out_ref, blocks_ref):
     line, across, high = blocks_ref.shape[0], blocks_ref.shape[1], blocks_ref.shape[2]
     cols = clip_ref.shape[1]
-    turned = clip_ref[0].T
+    total = clip_ref[0].astype(jnp.float32)
+    for s in range(1, clip_ref.shape[0]):
+        total = total + clip_ref[s].astype(jnp.float32)
+    turned = total.T
     blocks_ref[...] = jnp.zeros_like(blocks_ref)
     for z in range(across):
         for x in range(line):
@@ -284,7 +287,7 @@
     return kept.astype(jnp.float32) + lax.ppermute(sent, axis, moves).astype(jnp.float32)
 
 
-SEQ = ("zl", "y")
+SEQ = ("zl", "yh", "yl")
 ROWS = ("zh", "x")
 DP = ("zh", "x", "c")
 ROWS_DEV = 18
@@ -305,7 +308,7 @@
     tokens, _, width = qkv.shape
     seq_count = lax.axis_size(SEQ)
     row_count = lax.axis_size(ROWS)
-    ring = lax.axis_size("y")
+    ring = lax.axis_size(("yh", "yl"))
     rows, cols = w_master.shape
     core, side = lax.axis_index("c"), lax.axis_index("zl")
     core_id = core[None].astype(jnp.int32)
@@ -341,22 +344,17 @@
     row_block, quad = lax.optimization_barrier((row_block, quad))
     own = exchange(jnp.broadcast_to(row_block[None], (row_count,) + row_block.shape), ROWS)
     probs = probs_call(heads_qkv)
-    clip = halve(quad.reshape(ring, cols, quad.shape[1]), "y", 0)
+    clip = halve(quad.reshape(ring, cols, quad.shape[1]), "yl", 0)
     own, probs, near, clip = lax.optimization_barrier((own, probs, near, clip))
+    clip = exchange(clip.astype(jnp.bfloat16), "yh")
     own = own.reshape(row_count * SHARE, width)
     other = lax.ppermute(own, "c", SWAP)
     grad_rows = project_call(core_id, own, other, dout, near, seq_count)
+    grad_rows, clip = lax.optimization_barrier((grad_rows, clip))
     heads_grad = exchange(grad_rows, SEQ)
 
     line, across = lax.axis_size("x"), lax.axis_size("zh")
-    clip, _ = lax.optimization_barrier((clip, grad_rows))
-    step = lax.axis_index("y") // 2
-    total = at(clip, step)
-    for turn in range(1, ring // 2):
-        moves = [(i, (i + 2 * turn) % ring) for i in range(ring)]
-        sent = lax.ppermute(at(clip, (step + turn) % (ring // 2)).astype(jnp.bfloat16), "y", moves)
-        total = total + sent.astype(jnp.float32)
-    pieces = arrange_call(total[None], line, across)
+    pieces = arrange_call(clip, line, across)
     pieces, heads_grad, probs = lax.optimization_barrier((pieces, heads_grad, probs))
     pieces = exchange(pieces, "x")
     local = grads_call(heads_qkv, heads_grad, probs)
@@ -380,7 +378,7 @@
 
 
 def solution(mesh):
-    fine = Mesh(mesh.devices.reshape(4, 8, 2, 2, 8), ("zh", "x", "c", "zl", "y"))
+    fine = Mesh(mesh.devices.reshape(4, 8, 2, 2, 4, 2), DP + SEQ)
     rows = P(DP + SEQ)
     square = P(DP, SEQ)
     return jax.shard_map(

time: 194 us -> 192 us (0.990)
  the two profiles are of different devices: /device:TPU:1 before, /device:TPU:10 now
where the time goes in v5:
time: 192 us; the launch traced here: 191 us
  starting transfers between devices  86.2 us (45%)
  waiting for transfers between devices  59.3 us (31%)
  Pallas kernels  29.5 us (15%)
  local copies, waits for them, and re-layouts  8.48 us (4%)
  other arithmetic  6.78 us (4%)
    all_to_all x6, starting transfers between devices, exchange(): return lax.all_to_all(array, axes, 0, 0, tiled=True)  52.7 us
    all_to_all x6, waiting for transfers between devices, exchange(): return lax.all_to_all(array, axes, 0, 0, tiled=True)  41 us
    ppermute x4, starting transfers between devices, per_device(): lax.ppermute(at(pieces, (lax.axis_index('zh') + turn) % across), DP, moves)  18.7 us
    pallas_call x1, Pallas kernels, grads_call(): pl.pallas_call(grads_kernel, out_shape=jax.ShapeDtypeStruct(heads.shape,...  15 us
    ppermute x4, waiting for transfers between devices, per_device(): lax.ppermute(at(pieces, (lax.axis_index('zh') + turn) % across), DP, moves)  11.5 us
    pallas_call x1, Pallas kernels, probs_call(): pl.pallas_call(probs_kernel, out_shape=jax.ShapeDtypeStruct((length, leng...  9.79 us
    ppermute x1, starting transfers between devices, halve(): lax.ppermute(sent, axis, moves).astype(jnp.float32)  3.87 us
  transfers between devices with their start and end apart: 15, of which 7 were waited for; matrix products, arithmetic and copies ran while one was open for 4% of the time, Pallas kernels for 14%

profile of v5, /device:TPU:10, one launch (start us, length us, event | category | flops | bytes accessed | tf_op | source)
XLA Modules:
  0.0 191.1 jit_solution(6868749724631950133)
XLA Ops:
  0.6 1.4 fusion.2
  2.0 0.1 reshape.55
  2.1 1.8 copy.18
  4.0 0.0 copy-start
  4.0 0.0 copy-start.1
  4.0 0.1 copy.19
  4.1 1.0 pad_maximum_fusion
  5.1 1.8 term.1
  6.9 1.9 %collective-permute-start = (bf16[1152,640]{1,0:T(8,128)(2,1)S(1)}, bf16[1152,640]{1,0:T(8,128)(2,1)}, u32[]{:S(2)}, u32[]{:S(2)}) collective-permute-start(bf16[1152,640]{1,0:T(8,128)(2,1)S(1)} %get-tuple-element.27), channel_id=1, source_target_pairs={{0,16},{16,0},{1,17},{17,1},{2,18},{18,2},{3,19},{19,3},{4,20},{20... | collective-permute-start | bytes 4423688 | tf_op jit(solution)/shard_map/ppermute | solution.py:335
  8.8 10.4 %all-to-all-start = ((bf16[16,224,128]{2,1,0:T(8,128)(2,1)}), bf16[16,224,128]{2,1,0:T(8,128)(2,1)}, u32[]{:S(2)}, u32[]{:S(2)}) async-start(bf16[16,224,128]{2,1,0:T(8,128)(2,1)} %pad_maximum_fusion), calls=%async_computation | async-start | bytes 1835008 | tf_op jit(solution)/shard_map/all_to_all | solution.py:300
  19.3 1.7 add_convert_fusion
  21.1 0.1 dynamic-slice_bitcast_fusion
  21.1 3.8 %collective-permute-start.1 = (bf16[576,640]{1,0:T(8,128)(2,1)S(1)}, bf16[576,640]{1,0:T(8,128)(2,1)S(1)}, u32[]{:S(2)}, u32[]{:S(2)}) collective-permute-start(bf16[576,640]{1,0:T(8,128)(2,1)S(1)} %dynamic-slice_bitcast_fusion), channel_id=1, source_target_pairs={{0,8},{8,0},{1,9},{9,1},{2,10},{10,2},{3,11},{11,3},{4,12},{12,4},... | collective-permute-start | bytes 2211848 | tf_op jit(solution)/shard_map/ppermute | solution.py:338
  24.9 19.5 %all-to-all-done = bf16[16,224,128]{2,1,0:T(8,128)(2,1)} async-done(((bf16[16,224,128]{2,1,0:T(8,128)(2,1)}), bf16[16,224,128]{2,1,0:T(8,128)(2,1)}, u32[]{:S(2)}, u32[]{:S(2)}) %all-to-all-start) | async-done | bytes 917536 | tf_op jit(solution)/shard_map/all_to_all | solution.py:300
  44.4 0.8 slice.17
  45.2 0.1 reshape.59
  45.4 0.1 reshape.60
  45.5 3.7 %collective-permute-done.1 = bf16[576,640]{1,0:T(8,128)(2,1)S(1)} collective-permute-done((bf16[576,640]{1,0:T(8,128)(2,1)S(1)}, bf16[576,640]{1,0:T(8,128)(2,1)S(1)}, u32[]{:S(2)}, u32[]{:S(2)}) %collective-permute-start.1) | collective-permute-done | bytes 737312 | tf_op jit(solution)/shard_map/ppermute | solution.py:338
  49.2 0.2 fusion
  49.4 1.0 broadcast_in_dim.19
  50.4 20.4 %all-to-all-start.1 = ((bf16[32,81,128]{2,1,0:T(8,128)(2,1)}), bf16[32,81,128]{2,1,0:T(8,128)(2,1)S(1)}, u32[]{:S(2)}, u32[]{:S(2)}) async-start(bf16[32,81,128]{2,1,0:T(8,128)(2,1)} %broadcast_in_dim.19), calls=%async_computation.1 | async-start | bytes 1441792 | tf_op jit(solution)/shard_map/all_to_all | solution.py:300
  70.8 0.8 dynamic-slice_bitcast_fusion.1
  71.6 3.9 %collective-permute-start.3 = (bf16[4,72,640]{2,1,0:T(8,128)(2,1)}, bf16[4,72,640]{2,1,0:T(8,128)(2,1)}, u32[]{:S(2)}, u32[]{:S(2)}) collective-permute-start(bf16[4,72,640]{2,1,0:T(8,128)(2,1)} %dynamic-slice_bitcast_fusion.1), channel_id=1, source_target_pairs={{0,1},{1,0},{2,3},{3,2},{4,5},{5,4},{6,7},{7,6},{8,9},{9,8},{10,11... | collective-permute-start | bytes 1105928 | tf_op jit(solution)/shard_map/ppermute | solution.py:287
  75.4 3.2 %collective-permute-start.2 = (bf16[128,1152]{1,0:T(8,128)(2,1)S(1)}, bf16[128,1152]{1,0:T(8,128)(2,1)S(1)}, u32[]{:S(2)}, u32[]{:S(2)}) collective-permute-start(bf16[128,1152]{1,0:T(8,128)(2,1)S(1)} %copy-done.1), channel_id=1, source_target_pairs={{0,8},{8,0},{1,9},{9,1},{2,10},{10,2},{3,11},{11,3},{4,12},{12,4},... | collective-permute-start | bytes 884744 | tf_op jit(solution)/shard_map/ppermute | solution.py:343
  78.6 1.2 slice.16
  79.9 9.8 %probs.1.probs_ref = bf16[2048,2048]{1,0:T(8,128)(2,1)} custom-call(bf16[16,3,72,128]{3,2,1,0:T(8,128)(2,1)S(1)} %bitcast.42), custom_call_target="tpu_custom_call" | custom-call | flops 2147483648 | bytes 8388608 | tf_op jit(solution)/shard_map/probs/pallas_call | solution.py:123
  89.7 1.8 convert_add_fusion.1
  91.5 3.1 %collective-permute-done.2.near_ref = bf16[128,1152]{1,0:T(8,128)(2,1)S(1)} collective-permute-done((bf16[128,1152]{1,0:T(8,128)(2,1)S(1)}, bf16[128,1152]{1,0:T(8,128)(2,1)S(1)}, u32[]{:S(2)}, u32[]{:S(2)}) %collective-permute-start.2) | collective-permute-done | bytes 294944 | tf_op jit(solution)/shard_map/ppermute | solution.py:343
  94.6 0.8 reshape.62.own_ref
  95.4 1.9 %collective-permute-start.4 = (bf16[288,1152]{1,0:T(8,128)(2,1)S(1)}, bf16[288,1152]{1,0:T(8,128)(2,1)S(1)}, u32[]{:S(2)}, u32[]{:S(2)}) collective-permute-start(bf16[288,1152]{1,0:T(8,128)(2,1)S(1)} %reshape.62.own_ref), channel_id=1, source_target_pairs={{0,16},{16,0},{1,17},{17,1},{2,18},{18,2},{3,19},{19,3},{4,20},{20... | collective-permute-start | bytes 1990664 | tf_op jit(solution)/shard_map/ppermute | solution.py:351
  97.3 5.6 %all-to-all-start.2 = ((bf16[4,72,640]{2,1,0:T(8,128)(2,1)}), bf16[4,72,640]{2,1,0:T(8,128)(2,1)S(1)}, u32[]{:S(2)}, u32[]{:S(2)}) async-start(bf16[4,72,640]{2,1,0:T(8,128)(2,1)} %convert_add_fusion.1), calls=%async_computation.2 | async-start | bytes 737280 | tf_op jit(solution)/shard_map/all_to_all | solution.py:300
  102.9 1.9 %project.1 = bf16[16,80,128]{2,1,0:T(8,128)(2,1)} custom-call(s32[1]{0:T(128)} %bitcast.5.refs_0_.core_ref, bf16[288,1152]{1,0:T(8,128)(2,1)S(1)} %reshape.62.own_ref, bf16[288,1152]{1,0:T(8,128)(2,1)S(1)} %collective-permute-done.4.other_ref, bf16[128,1152]{1,0:T(8,128)(2,1)S(1)} %copy-done.1, bf16[128,1152]{1,0:T(8,128)(2,1)S(1)} %collective-permute-done.2.near_ref), custom_call_target="tpu_custom_call" | custom-call | flops 679477248 | bytes 5308416 | tf_op jit(solution)/shard_map/project/pallas_call | solution.py:237
  104.8 11.1 %all-to-all-done.2.clip_ref = bf16[4,72,640]{2,1,0:T(8,128)(2,1)S(1)} async-done(((bf16[4,72,640]{2,1,0:T(8,128)(2,1)}), bf16[4,72,640]{2,1,0:T(8,128)(2,1)S(1)}, u32[]{:S(2)}, u32[]{:S(2)}) %all-to-all-start.2) | async-done | bytes 368672 | tf_op jit(solution)/shard_map/all_to_all | solution.py:300
  115.9 5.4 %all-to-all-start.3 = ((bf16[16,80,128]{2,1,0:T(8,128)(2,1)}), bf16[16,80,128]{2,1,0:T(8,128)(2,1)S(1)}, u32[]{:S(2)}, u32[]{:S(2)}) async-start(bf16[16,80,128]{2,1,0:T(8,128)(2,1)} %project.1), calls=%async_computation.3 | async-start | bytes 655360 | tf_op jit(solution)/shard_map/all_to_all | solution.py:300
  121.3 0.9 arrange.1
  122.2 10.4 %all-to-all-done.3.grad_ref = bf16[16,80,128]{2,1,0:T(8,128)(2,1)S(1)} async-done(((bf16[16,80,128]{2,1,0:T(8,128)(2,1)}), bf16[16,80,128]{2,1,0:T(8,128)(2,1)S(1)}, u32[]{:S(2)}, u32[]{:S(2)}) %all-to-all-start.3) | async-done | bytes 327712 | tf_op jit(solution)/shard_map/all_to_all | solution.py:300
  132.5 6.3 %all-to-all-start.4 = ((bf16[8,96,128]{2,1,0:T(8,128)(2,1)}), bf16[8,96,128]{2,1,0:T(8,128)(2,1)S(1)}, u32[]{:S(2)}, u32[]{:S(2)}) async-start(bf16[8,96,128]{2,1,0:T(8,128)(2,1)} %arrange.1), calls=%async_computation.4 | async-start | bytes 393216 | tf_op jit(solution)/shard_map/all_to_all | solution.py:300
  138.8 15.0 %grads.1 = bf16[16,3,72,128]{3,2,1,0:T(8,128)(2,1)} custom-call(bf16[16,3,72,128]{3,2,1,0:T(8,128)(2,1)S(1)} %bitcast.43, bf16[16,80,128]{2,1,0:T(8,128)(2,1)S(1)} %all-to-all-done.3.grad_ref, bf16[2048,2048]{1,0:T(8,128)(2,1)} %probs.1.probs_ref), custom_call_target="tpu_custom_call" | custom-call | flops 8589934592 | bytes 8388608 | tf_op jit(solution)/shard_map/grads/pallas_call | solution.py:142
  153.9 4.6 %all-to-all-start.5 = ((bf16[16,3,72,128]{3,2,1,0:T(8,128)(2,1)}), bf16[16,3,72,128]{3,2,1,0:T(8,128)(2,1)S(1)}, u32[]{:S(2)}, u32[]{:S(2)}) async-start(bf16[16,3,72,128]{3,2,1,0:T(8,128)(2,1)} %grads.1), calls=%async_computation.5 | async-start | bytes 1769472 | tf_op jit(solution)/shard_map/all_to_all | solution.py:300
  158.7 1.9 %collective-permute-start.5 = (f32[24,128]{1,0:T(8,128)S(1)}, f32[24,128]{1,0:T(8,128)S(1)}, u32[]{:S(2)}, u32[]{:S(2)}) collective-permute-start(f32[24,128]{1,0:T(8,128)S(1)} %get-tuple-element.55), channel_id=1, source_target_pairs={{0,0},{16,512},{32,16},{48,528},{64,32},{80,544},{96,48},{112,560}... | collective-permute-start | bytes 36872 | tf_op jit(solution)/shard_map/ppermute | solution.py:372
  160.6 8.1 %collective-permute-start.6 = (f32[24,128]{1,0:T(8,128)S(1)}, f32[24,128]{1,0:T(8,128)S(1)}, u32[]{:S(2)}, u32[]{:S(2)}) collective-permute-start(f32[24,128]{1,0:T(8,128)S(1)} %get-tuple-element.58), channel_id=1, source_target_pairs={{0,128},{16,640},{32,144},{48,656},{64,160},{80,672},{96,176},{112... | collective-permute-start | bytes 36872 | tf_op jit(solution)/shard_map/ppermute | solution.py:372
  168.7 6.9 %collective-permute-start.7 = (f32[24,128]{1,0:T(8,128)S(1)}, f32[24,128]{1,0:T(8,128)S(1)}, u32[]{:S(2)}, u32[]{:S(2)}) collective-permute-start(f32[24,128]{1,0:T(8,128)S(1)} %get-tuple-element.57), channel_id=1, source_target_pairs={{0,256},{16,768},{32,272},{48,784},{64,288},{80,800},{96,304},{112... | collective-permute-start | bytes 36872 | tf_op jit(solution)/shard_map/ppermute | solution.py:372
  175.5 1.9 %collective-permute-start.8 = (f32[24,128]{1,0:T(8,128)S(1)}, f32[24,128]{1,0:T(8,128)S(1)}, u32[]{:S(2)}, u32[]{:S(2)}) collective-permute-start(f32[24,128]{1,0:T(8,128)S(1)} %get-tuple-element.56), channel_id=1, source_target_pairs={{0,384},{16,896},{32,400},{48,912},{64,416},{80,928},{96,432},{112... | collective-permute-start | bytes 36872 | tf_op jit(solution)/shard_map/ppermute | solution.py:372
  177.5 2.9 %collective-permute-done.7 = f32[24,128]{1,0:T(8,128)S(1)} collective-permute-done((f32[24,128]{1,0:T(8,128)S(1)}, f32[24,128]{1,0:T(8,128)S(1)}, u32[]{:S(2)}, u32[]{:S(2)}) %collective-permute-start.7) | collective-permute-done | bytes 12320 | tf_op jit(solution)/shard_map/ppermute | solution.py:372
  180.4 8.5 %collective-permute-done.8 = f32[24,128]{1,0:T(8,128)S(1)} collective-permute-done((f32[24,128]{1,0:T(8,128)S(1)}, f32[24,128]{1,0:T(8,128)S(1)}, u32[]{:S(2)}, u32[]{:S(2)}) %collective-permute-start.8) | collective-permute-done | bytes 12320 | tf_op jit(solution)/shard_map/ppermute | solution.py:372
  188.9 0.6 slice_add_fusion
  189.5 0.1 copy.22
  189.6 1.5 copy.23
  (18 shorter events, 0.1 us)
Async XLA Ops:
  4.0 1.1 copy-start
  4.0 1.1 copy-start.1
  6.9 12.4 %collective-permute-start = (bf16[1152,640]{1,0:T(8,128)(2,1)S(1)}, bf16[1152,640]{1,0:T(8,128)(2,1)}, u32[]{:S(2)}, u32[]{:S(2)}) collective-permute-start(bf16[1152,640]{1,0:T(8,128)(2,1)S(1)} %get-tuple-element.27), channel_id=1, source_target_pairs={{0,16},{16,0},{1,17},{17,1},{2,18},{18,2},{3,19},{19,3},{4,20},{20... | collective-permute-start | bytes 4423688 | tf_op jit(solution)/shard_map/ppermute | solution.py:335
  8.8 35.6 %all-to-all-start = ((bf16[16,224,128]{2,1,0:T(8,128)(2,1)}), bf16[16,224,128]{2,1,0:T(8,128)(2,1)}, u32[]{:S(2)}, u32[]{:S(2)}) async-start(bf16[16,224,128]{2,1,0:T(8,128)(2,1)} %pad_maximum_fusion), calls=%async_computation | async-start | bytes 1835008 | tf_op jit(solution)/shard_map/all_to_all | solution.py:300
  21.1 28.1 %collective-permute-start.1 = (bf16[576,640]{1,0:T(8,128)(2,1)S(1)}, bf16[576,640]{1,0:T(8,128)(2,1)S(1)}, u32[]{:S(2)}, u32[]{:S(2)}) collective-permute-start(bf16[576,640]{1,0:T(8,128)(2,1)S(1)} %dynamic-slice_bitcast_fusion), channel_id=1, source_target_pairs={{0,8},{8,0},{1,9},{9,1},{2,10},{10,2},{3,11},{11,3},{4,12},{12,4},... | collective-permute-start | bytes 2211848 | tf_op jit(solution)/shard_map/ppermute | solution.py:338
  50.4 44.2 %all-to-all-start.1 = ((bf16[32,81,128]{2,1,0:T(8,128)(2,1)}), bf16[32,81,128]{2,1,0:T(8,128)(2,1)S(1)}, u32[]{:S(2)}, u32[]{:S(2)}) async-start(bf16[32,81,128]{2,1,0:T(8,128)(2,1)} %broadcast_in_dim.19), calls=%async_computation.1 | async-start | bytes 1441792 | tf_op jit(solution)/shard_map/all_to_all | solution.py:300
  71.6 18.1 %collective-permute-start.3 = (bf16[4,72,640]{2,1,0:T(8,128)(2,1)}, bf16[4,72,640]{2,1,0:T(8,128)(2,1)}, u32[]{:S(2)}, u32[]{:S(2)}) collective-permute-start(bf16[4,72,640]{2,1,0:T(8,128)(2,1)} %dynamic-slice_bitcast_fusion.1), channel_id=1, source_target_pairs={{0,1},{1,0},{2,3},{3,2},{4,5},{5,4},{6,7},{7,6},{8,9},{9,8},{10,11... | collective-permute-start | bytes 1105928 | tf_op jit(solution)/shard_map/ppermute | solution.py:287
  75.4 19.1 %collective-permute-start.2 = (bf16[128,1152]{1,0:T(8,128)(2,1)S(1)}, bf16[128,1152]{1,0:T(8,128)(2,1)S(1)}, u32[]{:S(2)}, u32[]{:S(2)}) collective-permute-start(bf16[128,1152]{1,0:T(8,128)(2,1)S(1)} %copy-done.1), channel_id=1, source_target_pairs={{0,8},{8,0},{1,9},{9,1},{2,10},{10,2},{3,11},{11,3},{4,12},{12,4},... | collective-permute-start | bytes 884744 | tf_op jit(solution)/shard_map/ppermute | solution.py:343
  95.4 7.5 %collective-permute-start.4 = (bf16[288,1152]{1,0:T(8,128)(2,1)S(1)}, bf16[288,1152]{1,0:T(8,128)(2,1)S(1)}, u32[]{:S(2)}, u32[]{:S(2)}) collective-permute-start(bf16[288,1152]{1,0:T(8,128)(2,1)S(1)} %reshape.62.own_ref), channel_id=1, source_target_pairs={{0,16},{16,0},{1,17},{17,1},{2,18},{18,2},{3,19},{19,3},{4,20},{20... | collective-permute-start | bytes 1990664 | tf_op jit(solution)/shard_map/ppermute | solution.py:351
  97.3 18.6 %all-to-all-start.2 = ((bf16[4,72,640]{2,1,0:T(8,128)(2,1)}), bf16[4,72,640]{2,1,0:T(8,128)(2,1)S(1)}, u32[]{:S(2)}, u32[]{:S(2)}) async-start(bf16[4,72,640]{2,1,0:T(8,128)(2,1)} %convert_add_fusion.1), calls=%async_computation.2 | async-start | bytes 737280 | tf_op jit(solution)/shard_map/all_to_all | solution.py:300
  115.9 16.6 %all-to-all-start.3 = ((bf16[16,80,128]{2,1,0:T(8,128)(2,1)}), bf16[16,80,128]{2,1,0:T(8,128)(2,1)S(1)}, u32[]{:S(2)}, u32[]{:S(2)}) async-start(bf16[16,80,128]{2,1,0:T(8,128)(2,1)} %project.1), calls=%async_computation.3 | async-start | bytes 655360 | tf_op jit(solution)/shard_map/all_to_all | solution.py:300
  132.5 21.4 %all-to-all-start.4 = ((bf16[8,96,128]{2,1,0:T(8,128)(2,1)}), bf16[8,96,128]{2,1,0:T(8,128)(2,1)S(1)}, u32[]{:S(2)}, u32[]{:S(2)}) async-start(bf16[8,96,128]{2,1,0:T(8,128)(2,1)} %arrange.1), calls=%async_computation.4 | async-start | bytes 393216 | tf_op jit(solution)/shard_map/all_to_all | solution.py:300
  153.9 35.6 %all-to-all-start.5 = ((bf16[16,3,72,128]{3,2,1,0:T(8,128)(2,1)}), bf16[16,3,72,128]{3,2,1,0:T(8,128)(2,1)S(1)}, u32[]{:S(2)}, u32[]{:S(2)}) async-start(bf16[16,3,72,128]{3,2,1,0:T(8,128)(2,1)} %grads.1), calls=%async_computation.5 | async-start | bytes 1769472 | tf_op jit(solution)/shard_map/all_to_all | solution.py:300
  158.7 18.8 %collective-permute-start.5 = (f32[24,128]{1,0:T(8,128)S(1)}, f32[24,128]{1,0:T(8,128)S(1)}, u32[]{:S(2)}, u32[]{:S(2)}) collective-permute-start(f32[24,128]{1,0:T(8,128)S(1)} %get-tuple-element.55), channel_id=1, source_target_pairs={{0,0},{16,512},{32,16},{48,528},{64,32},{80,544},{96,48},{112,560}... | collective-permute-start | bytes 36872 | tf_op jit(solution)/shard_map/ppermute | solution.py:372
  160.6 16.9 %collective-permute-start.6 = (f32[24,128]{1,0:T(8,128)S(1)}, f32[24,128]{1,0:T(8,128)S(1)}, u32[]{:S(2)}, u32[]{:S(2)}) collective-permute-start(f32[24,128]{1,0:T(8,128)S(1)} %get-tuple-element.58), channel_id=1, source_target_pairs={{0,128},{16,640},{32,144},{48,656},{64,160},{80,672},{96,176},{112... | collective-permute-start | bytes 36872 | tf_op jit(solution)/shard_map/ppermute | solution.py:372
  168.7 11.7 %collective-permute-start.7 = (f32[24,128]{1,0:T(8,128)S(1)}, f32[24,128]{1,0:T(8,128)S(1)}, u32[]{:S(2)}, u32[]{:S(2)}) collective-permute-start(f32[24,128]{1,0:T(8,128)S(1)} %get-tuple-element.57), channel_id=1, source_target_pairs={{0,256},{16,768},{32,272},{48,784},{64,288},{80,800},{96,304},{112... | collective-permute-start | bytes 36872 | tf_op jit(solution)/shard_map/ppermute | solution.py:372
  175.5 13.4 %collective-permute-start.8 = (f32[24,128]{1,0:T(8,128)S(1)}, f32[24,128]{1,0:T(8,128)S(1)}, u32[]{:S(2)}, u32[]{:S(2)}) collective-permute-start(f32[24,128]{1,0:T(8,128)S(1)} %get-tuple-element.56), channel_id=1, source_target_pairs={{0,384},{16,896},{32,400},{48,912},{64,416},{80,928},{96,432},{112... | collective-permute-start | bytes 36872 | tf_op jit(solution)/shard_map/ppermute | solution.py:372
